TPU v7x, 256 devices: a whole 4x4x8 slice. The times are simulated.
256 devices in a mesh: seq: 64 (over z, y, core), tp: 4 (over x).
Axes of the slice: x: 4, y: 4, z: 8, core: 2. Of those that a mesh axis runs over, the one named last changes fastest.
Arguments:
- normed: bfloat16 [32768, 2048], P('seq', 'tp'), may hold values from -24 to 24
- cluster: int32 [32768, 1], P('seq'), may hold values from 0 to 127; in each aligned block of 512 rows (0 to 511, 512 to 1023, ...) at most 8 rows name the same one
- w_query: bfloat16 [2048, 2048], P(None, 'tp'), may hold values from -1 to 1
- w_key: bfloat16 [2048, 2048], P(None, 'tp'), may hold values from -1 to 1
- w_value: bfloat16 [2048, 2048], P(None, 'tp'), may hold values from -0.125 to 0.125
- w_out: bfloat16 [2048, 2048], P('tp'), may hold values from -0.125 to 0.125
- grad_out: bfloat16 [32768, 2048], P('seq', 'tp'), may hold values from -6 to 6
Outputs:
- attended: bfloat16 [32768, 2048], P('seq', 'tp')
- grad_normed: float32 [32768, 2048], P('seq', 'tp')
Inputs may be any that keep to these rules, and one draw needn't show every extreme that they name: Among the tokens of one index of seq no cluster id appears more than 8 times, and some id appears exactly 8 times; every id appears somewhere.
All inputs are finite; a program needn't handle non-finite values.
Results may differ from a plain program's by a relative error of at most 0.011.
The roundings to bfloat16 on the way count: a program that leaves them out, or rounds other values in their place, can miss the bound.
Values may be sent and summed in bfloat16 or wider, within the bound.
A program may use at most 128 MiB of HBM per device.

v0:
```python
import jax
import jax.numpy as jnp
from jax import lax
from jax.sharding import PartitionSpec as P

HEAD_DIM = 128
CLUSTERS = 128
CAP = 256
MOST = 8


def entering(x, axis, combine, identity):
    count, position = (lax.axis_size(axis), lax.axis_index(axis))
    everything = lax.all_gather(x, axis)
    start = jnp.broadcast_to(jnp.asarray(identity, x.dtype), x.shape)

    def lap(k, before):
        reached = k < position
        new = combine(before, everything[k])
        return jnp.where(reached, new, before)

    return lax.fori_loop(0, count, lap, start)


def cluster_probs(query, key_rows, usable):
    score_scale = query.shape[-1] ** (-0.5)
    scores = (
        jnp.einsum("qhd,khd->hqk", query, key_rows, preferred_element_type=jnp.float32)
        * score_scale
    )
    scores = jnp.where(usable[None, None, :], scores, -1e30)
    row_top = jnp.max(scores, axis=-1, keepdims=True)
    raised = jnp.exp(scores - row_top)
    return raised / jnp.sum(raised, axis=-1, keepdims=True)


def unpack(packed):
    width = packed.shape[1] // 3
    rows = packed.shape[0]
    query = packed[:, :width].reshape(rows, -1, HEAD_DIM)
    key_rows = packed[:, width : 2 * width].reshape(rows, -1, HEAD_DIM)
    value_rows = packed[:, 2 * width :].reshape(rows, -1, HEAD_DIM)
    return (query, key_rows, value_rows)


def forward_one(packed, usable):
    query, key_rows, value_rows = unpack(packed)
    probs = cluster_probs(query, key_rows, usable)
    mixed = jnp.einsum(
        "hqk,khd->qhd", probs.astype(jnp.bfloat16), value_rows, preferred_element_type=jnp.float32
    )
    return mixed.reshape(packed.shape[0], -1).astype(jnp.bfloat16)


def attention_core(packed, usable, grad_rows):
    query, key_rows, value_rows = unpack(packed)
    rows = packed.shape[0]
    score_scale = query.shape[-1] ** (-0.5)
    grad_heads = grad_rows.reshape(rows, -1, HEAD_DIM)
    probs = cluster_probs(query, key_rows, usable)
    rounded = probs.astype(jnp.bfloat16)
    mixed = jnp.einsum("hqk,khd->qhd", rounded, value_rows, preferred_element_type=jnp.float32)
    grad_value = jnp.einsum("hqk,qhd->khd", rounded, grad_heads, preferred_element_type=jnp.float32)
    grad_probs = jnp.einsum(
        "qhd,khd->hqk", grad_heads, value_rows, preferred_element_type=jnp.float32
    )
    inner = jnp.sum(grad_probs * probs, axis=-1, keepdims=True)
    grad_scores = (probs * (grad_probs - inner) * score_scale).astype(jnp.bfloat16)
    grad_query = jnp.einsum(
        "hqk,khd->qhd", grad_scores, key_rows, preferred_element_type=jnp.float32
    )
    grad_key = jnp.einsum("hqk,qhd->khd", grad_scores, query, preferred_element_type=jnp.float32)
    grads = jnp.concatenate(
        [
            grad_query.reshape(rows, -1).astype(jnp.bfloat16),
            grad_key.reshape(rows, -1).astype(jnp.bfloat16),
            grad_value.reshape(rows, -1).astype(jnp.bfloat16),
        ],
        axis=1,
    )
    return (mixed.reshape(rows, -1).astype(jnp.bfloat16), grads)


def body(normed, cluster, w_query, w_key, w_value, w_out, grad_out):
    seq_count = lax.axis_size("seq")
    local_cols = w_query.shape[1]
    cluster_here = CLUSTERS // seq_count
    cluster_ids = cluster[:, 0]
    columns = jnp.arange(CLUSTERS, dtype=jnp.int32)
    one_hot = (cluster_ids[:, None] == columns[None, :]).astype(jnp.int32)
    running = jnp.cumsum(one_hot, axis=0)
    local_rank = jnp.sum((running - one_hot) * one_hot, axis=1)
    counts = running[-1]
    offsets = entering(
        counts, "seq", lambda earlier, later: earlier + later, jnp.zeros_like(counts)
    )
    global_rank = local_rank + jnp.sum(one_hot * offsets[None, :], axis=1)
    kept_rows = (global_rank < CAP).astype(jnp.bfloat16)
    slot_index = cluster_ids * MOST + local_rank
    piece = lax.all_gather(normed, "tp", axis=1, tiled=True)
    query_sum = jnp.dot(piece, w_query, preferred_element_type=jnp.float32)
    key_sum = jnp.dot(piece, w_key, preferred_element_type=jnp.float32)
    value_sum = jnp.dot(piece, w_value, preferred_element_type=jnp.float32)
    packed_rows = jnp.concatenate(
        [
            query_sum.astype(jnp.bfloat16),
            key_sum.astype(jnp.bfloat16),
            value_sum.astype(jnp.bfloat16),
        ],
        axis=1,
    )
    head_grads = (
        lax.dot_general(
            lax.all_gather(grad_out, "tp", axis=1, tiled=True),
            w_out,
            (((1,), (1,)), ((), ())),
            preferred_element_type=jnp.float32,
        ).astype(jnp.bfloat16)
        * kept_rows[:, None]
    )

    def to_owners(rows):
        buffer = jnp.zeros((CLUSTERS * MOST, rows.shape[1]), rows.dtype).at[slot_index].set(rows)
        return buffer.reshape(seq_count, cluster_here, MOST, rows.shape[1])

    flags = (
        jnp.zeros((CLUSTERS * MOST,), jnp.bfloat16)
        .at[slot_index]
        .set(kept_rows)
        .reshape(seq_count, cluster_here, MOST)
    )

    def from_owners(slots):
        return slots.reshape(cluster_here, seq_count, MOST, slots.shape[-1])

    def to_tokens(returned):
        return (
            returned.reshape(CLUSTERS * MOST, returned.shape[-1])[slot_index] * kept_rows[:, None]
        )

    arrived, arrived_flags = (
        lax.all_to_all(to_owners(packed_rows), "seq", split_axis=0, concat_axis=2, tiled=True),
        lax.all_to_all(flags, "seq", split_axis=0, concat_axis=2, tiled=True),
    )
    usable = arrived_flags[0] > 0
    mixed_slots = lax.map(lambda pair: forward_one(pair[0], pair[1]), (arrived[0], usable))
    heads_tok = to_tokens(
        lax.all_to_all(from_owners(mixed_slots), "seq", split_axis=1, concat_axis=0, tiled=True)
    )
    grad_arrived = lax.all_to_all(
        to_owners(head_grads), "seq", split_axis=0, concat_axis=2, tiled=True
    )
    grad_slots = lax.map(
        lambda triple: attention_core(triple[0], triple[1], triple[2])[1],
        (arrived[0], usable, grad_arrived[0]),
    )
    grads_tok = to_tokens(
        lax.all_to_all(from_owners(grad_slots), "seq", split_axis=1, concat_axis=0, tiled=True)
    )
    partial_out = jnp.dot(heads_tok, w_out, preferred_element_type=jnp.float32)
    attended = lax.psum_scatter(partial_out, "tp", scatter_dimension=1, tiled=True).astype(
        jnp.bfloat16
    )
    contract = (((1,), (1,)), ((), ()))
    partial_grad = lax.dot_general(
        grads_tok[:, :local_cols], w_query, contract, preferred_element_type=jnp.float32
    )
    partial_grad = partial_grad + lax.dot_general(
        grads_tok[:, local_cols : 2 * local_cols],
        w_key,
        contract,
        preferred_element_type=jnp.float32,
    )
    partial_grad = partial_grad + lax.dot_general(
        grads_tok[:, 2 * local_cols :], w_value, contract, preferred_element_type=jnp.float32
    )
    grad_normed = lax.psum_scatter(partial_grad, "tp", scatter_dimension=1, tiled=True)
    return (attended, grad_normed)


def solution(mesh):
    in_specs = (
        P("seq", "tp"),
        P("seq", None),
        P(None, "tp"),
        P(None, "tp"),
        P(None, "tp"),
        P("tp", None),
        P("seq", "tp"),
    )
    out_specs = (P("seq", "tp"), P("seq", "tp"))
    return jax.shard_map(body, mesh=mesh, in_specs=in_specs, out_specs=out_specs, check_vma=False)
```

profile of v0, /device:TPU:1, one launch (start us, length us, event | category | flops | bytes accessed | tf_op | source)
XLA Modules:
  0.0 460.6 jit_solution(15803309775498486307)
XLA Ops:
  9.0 44.2 %all-gather = s32[64,1,128]{2,1,0:T(1,128)S(1)} all-gather(s32[1,1,128]{2,1,0:T(1,128)S(1)} %slice_bitcast_fusion.1), channel_id=1, replica_groups=mesh['seq'=64,'tp'=4] {'seq'}, dimensions={0}, use_global_device_ids=true | all-gather | bytes 33280 | tf_op jit(solution)/shard_map/all_gather | solution.py:14
  57.5 3.8 scatter_custom_fusion.1
  62.0 7.1 %all-to-all-start.1 = ((bf16[64,2,8]{2,1,0:T(2,128)(2,1)}), bf16[64,2,8]{2,1,0:T(2,128)(2,1)S(1)}, u32[]{:S(2)}, u32[]{:S(2)}) async-start(bf16[64,2,8]{2,1,0:T(2,128)(2,1)} %reshape.110), calls=%async_computation.1 | async-start | bytes 65536 | tf_op jit(solution)/shard_map/all_to_all | solution.py:143
  69.2 3.7 convolution_convert_fusion.1
  79.6 6.0 %scatter_custom_fusion = bf16[1024,1536]{1,0:T(8,128)(2,1)} fusion(s32[512]{0:T(512)S(1)} %bitcast.181, bf16[512,1536]{1,0:T(8,128)(2,1)} %copy.73, bf16[]{:T(256)} %constant.82.clone.1), kind=kCustom, calls=%fused_computation.59 | custom fusion | bytes 3146240 | tf_op jit(solution)/shard_map/scatter | solution.py:123
  85.6 10.5 %all-to-all-start = ((bf16[64,2,8,1536]{3,2,1,0:T(8,128)(2,1)}), bf16[64,2,8,1536]{3,2,1,0:T(8,128)(2,1)}, u32[]{:S(2)}, u32[]{:S(2)}) async-start(bf16[64,2,8,1536]{3,2,1,0:T(8,128)(2,1)} %bitcast.169), calls=%async_computation | async-start | bytes 6291456 | tf_op jit(solution)/shard_map/all_to_all | solution.py:142
  97.0 36.1 %all-gather.6.cloned.1.call-done = bf16[512,2048]{1,0:T(8,128)(2,1)} async-done(((bf16[512,512]{1,0:T(8,128)(2,1)}), bf16[512,2048]{1,0:T(8,128)(2,1)}) %all-gather.6.cloned.1.call-update) | async-done | bytes 2097168 | tf_op jit(solution)/shard_map/all_gather | solution.py:114
  135.9 3.5 scatter_custom_fusion.2
  139.4 29.1 %all-to-all-done = bf16[64,2,8,1536]{3,2,1,0:T(8,128)(2,1)} async-done(((bf16[64,2,8,1536]{3,2,1,0:T(8,128)(2,1)}), bf16[64,2,8,1536]{3,2,1,0:T(8,128)(2,1)}, u32[]{:S(2)}, u32[]{:S(2)}) %all-to-all-start) | async-done | bytes 3145760 | tf_op jit(solution)/shard_map/all_to_all | solution.py:142
  168.6 6.8 %all-to-all-start.3 = ((bf16[64,2,8,512]{3,2,1,0:T(8,128)(2,1)}), bf16[64,2,8,512]{3,2,1,0:T(8,128)(2,1)}, u32[]{:S(2)}, u32[]{:S(2)}) async-start(bf16[64,2,8,512]{3,2,1,0:T(8,128)(2,1)} %bitcast.38), calls=%async_computation.4 | async-start | bytes 2097152 | tf_op jit(solution)/shard_map/all_to_all | solution.py:150
  175.4 3.8 copy_bitcast_fusion
  179.2 4.7 %copy.76 = bf16[2,512,1536]{1,2,0:T(8,128)(2,1)} copy(bf16[2,512,1536]{2,1,0:T(8,128)(2,1)} %copy_bitcast_fusion) | data formatting | bytes 6291456 | tf_op jit(solution)/shard_map/while | solution.py:146
  183.9 21.6 %while.34 = (s32[]{:T(128)}, bf16[2,512,512]{2,1,0:T(8,128)(2,1)}, bf16[2,512,1536]{1,2,0:T(8,128)(2,1)}, pred[2,512]{1,0:T(4,128)(4,1)S(1)}, s32[]{:T(128)}) while((s32[]{:T(128)}, bf16[2,512,512]{2,1,0:T(8,128)(2,1)}, bf16[2,512,1536]{1,2,0:T(8,128)(2,1)}, pred[2,512]{1,0:T(4,128)(4,1)S(1)}, s32[]{:T(128)}) %tuple.85), condition=%wide.region_11.12_spmd, body=%wide.region_8.11_spmd.sunk | while | flops 543425024 | bytes 18892868 | solution.py:146
  186.3 4.7 %fusion.125 = (f32[4,512]{1,0:T(4,128)S(1)}, f32[4,512,512]{1,2,0:T(8,128)}) fusion(pred[512]{0:T(512)(128)(4,1)S(1)} %dynamic-slice_reduce_fusion.4, bf16[512,4,128]{0,2,1:T(8,128)(2,1)} %bitcast.166, bf16[512,4,128]{0,2,1:T(8,128)(2,1)S(1)} %bitcast.165), kind=kOutput, calls=%fused_computation.96.clone.1 | convolution fusion | flops 272630272 | bytes 5251584 | tf_op jit(solution)/shard_map/while/body/eval_jaxpr/sub | solution.py:33
  197.1 4.7 %fusion.125 = (f32[4,512]{1,0:T(4,128)S(1)}, f32[4,512,512]{1,2,0:T(8,128)}) fusion(pred[512]{0:T(512)(128)(4,1)S(1)} %dynamic-slice_reduce_fusion.4, bf16[512,4,128]{0,2,1:T(8,128)(2,1)} %bitcast.166, bf16[512,4,128]{0,2,1:T(8,128)(2,1)S(1)} %bitcast.165), kind=kOutput, calls=%fused_computation.96.clone.1 | convolution fusion | flops 272630272 | bytes 5251584 | tf_op jit(solution)/shard_map/while/body/eval_jaxpr/sub | solution.py:33
  207.9 10.3 %all-to-all-start.2 = ((bf16[2,64,8,512]{3,2,0,1:T(8,128)(2,1)}), bf16[2,64,8,512]{3,2,0,1:T(8,128)(2,1)S(1)}, u32[]{:S(2)}, u32[]{:S(2)}) async-start(bf16[2,64,8,512]{3,2,0,1:T(8,128)(2,1)} %copy.78), calls=%async_computation.2 | async-start | bytes 2097152 | tf_op jit(solution)/shard_map/all_to_all | solution.py:148
  220.6 25.6 %all-to-all-done.2 = bf16[2,64,8,512]{3,2,0,1:T(8,128)(2,1)S(1)} async-done(((bf16[2,64,8,512]{3,2,0,1:T(8,128)(2,1)}), bf16[2,64,8,512]{3,2,0,1:T(8,128)(2,1)S(1)}, u32[]{:S(2)}, u32[]{:S(2)}) %all-to-all-start.2) | async-done | bytes 1048608 | tf_op jit(solution)/shard_map/all_to_all | solution.py:148
  248.8 4.3 fusion.57
  253.4 60.3 %while.35 = (s32[]{:T(128)}, bf16[2,512,1536]{2,1,0:T(8,128)(2,1)}, bf16[2,512,1536]{1,2,0:T(8,128)(2,1)}, pred[2,512]{1,0:T(4,128)(4,1)S(1)}, bf16[2,512,512]{2,1,0:T(8,128)(2,1)}, /*index=5*/s32[]{:T(128)}) while((s32[]{:T(128)}, bf16[2,512,1536]{2,1,0:T(8,128)(2,1)}, bf16[2,512,1536]{1,2,0:T(8,128)(2,1)}, pred[2,512]{1,0:T(4,128)(4,1)S(1)}, ...), condition=%wide.region_18.19_spmd, body=%wide.region_14.18_spmd.sunk | while | flops 1368659456 | bytes 52463696 | solution.py:153
  255.1 3.7 fusion.138
  260.0 2.9 fusion.140
  263.0 7.8 %fusion.142 = bf16[4,128,512]{2,1,0:T(8,128)(2,1)S(1)} fusion(bf16[512,4,128]{0,2,1:T(8,128)(2,1)S(1)} %bitcast.162, f32[4,512,512]{1,2,0:T(8,128)} %fusion.140, f32[4,512,512]{1,2,0:T(8,128)} %get-tuple-element.302, f32[4,512]{1,0:T(4,128)S(1)} %get-tuple-element.303), kind=kOutput, calls=%fused_computation.44.clone.1 | convolution fusion | flops 276040192 | bytes 9445376 | tf_op jit(solution)/shard_map/while/body/eval_jaxpr/hqk,khd->qhd/dot_general | solution.py:69
  270.8 7.7 %fusion.141 = bf16[4,128,512]{2,1,0:T(8,128)(2,1)S(1)} fusion(bf16[512,4,128]{0,2,1:T(8,128)(2,1)S(1)} %bitcast.160, f32[4,512,512]{1,2,0:T(8,128)} %fusion.140, f32[4,512,512]{1,2,0:T(8,128)} %get-tuple-element.302, f32[4,512]{1,0:T(4,128)S(1)} %get-tuple-element.303), kind=kOutput, calls=%fused_computation.45.clone.1 | convolution fusion | flops 276040192 | bytes 9445376 | tf_op jit(solution)/shard_map/while/body/eval_jaxpr/hqk,qhd->khd/dot_general | solution.py:72
  278.5 3.1 fusion.139
  285.3 3.7 fusion.138
  293.0 7.9 %fusion.142 = bf16[4,128,512]{2,1,0:T(8,128)(2,1)S(1)} fusion(bf16[512,4,128]{0,2,1:T(8,128)(2,1)S(1)} %bitcast.162, f32[4,512,512]{1,2,0:T(8,128)} %fusion.140, f32[4,512,512]{1,2,0:T(8,128)} %get-tuple-element.302, f32[4,512]{1,0:T(4,128)S(1)} %get-tuple-element.303), kind=kOutput, calls=%fused_computation.44.clone.1 | convolution fusion | flops 276040192 | bytes 9445376 | tf_op jit(solution)/shard_map/while/body/eval_jaxpr/hqk,khd->qhd/dot_general | solution.py:69
  300.9 7.6 %fusion.141 = bf16[4,128,512]{2,1,0:T(8,128)(2,1)S(1)} fusion(bf16[512,4,128]{0,2,1:T(8,128)(2,1)S(1)} %bitcast.160, f32[4,512,512]{1,2,0:T(8,128)} %fusion.140, f32[4,512,512]{1,2,0:T(8,128)} %get-tuple-element.302, f32[4,512]{1,0:T(4,128)S(1)} %get-tuple-element.303), kind=kOutput, calls=%fused_computation.45.clone.1 | convolution fusion | flops 276040192 | bytes 9445376 | tf_op jit(solution)/shard_map/while/body/eval_jaxpr/hqk,qhd->khd/dot_general | solution.py:72
  308.5 3.0 fusion.139
  316.0 79.5 %all_to_all.69 = bf16[2,64,8,1536]{3,2,0,1:T(8,128)(2,1)S(1)} all-to-all(bf16[2,64,8,1536]{3,2,0,1:T(8,128)(2,1)S(1)} %copy.83), channel_id=1, replica_groups=mesh['seq'=64,'tp'=4] {'seq'}, dimensions={1} | all-to-all | bytes 6291456 | tf_op jit(solution)/shard_map/all_to_all | solution.py:158
  395.5 3.0 gather_fusion.1
  403.7 3.3 add_add_fusion
  409.1 44.7 %reduce-scatter.5.cloned.1.call-done = f32[512,512]{1,0:T(8,128)} async-done(((f32[512,2048]{1,0:T(8,128)}), f32[512,512]{1,0:T(8,128)}) %reduce-scatter.5.cloned.1.call-update) | async-done | bytes 1048592 | tf_op jit(solution)/shard_map/reduce_scatter | solution.py:177
  (155 shorter events, 60.8 us)
Async XLA Ops:
  7.2 125.9 %copy-start = (bf16[512,2048]{1,0:T(8,128)(2,1)S(1)}, bf16[512,2048]{1,0:T(8,128)(2,1)}, u32[]{:S(2)}) copy-start(bf16[512,2048]{1,0:T(8,128)(2,1)} %param.18) | copy-start | bytes 6291460
  7.2 61.9 %all-gather.4.cloned.1.call-start = ((), (), s32[]{:S(2)}) async-start(), calls=%async_computation.7 | async-start | bytes 2621440 | tf_op jit(solution)/shard_map/all_gather | solution.py:100
  62.0 23.6 %all-to-all-start.1 = ((bf16[64,2,8]{2,1,0:T(2,128)(2,1)}), bf16[64,2,8]{2,1,0:T(2,128)(2,1)S(1)}, u32[]{:S(2)}, u32[]{:S(2)}) async-start(bf16[64,2,8]{2,1,0:T(2,128)(2,1)} %reshape.110), calls=%async_computation.1 | async-start | bytes 65536 | tf_op jit(solution)/shard_map/all_to_all | solution.py:143
  69.1 3.7 copy-start.2
  69.1 3.7 copy-start.7
  72.9 1.6 copy-start.4
  85.6 83.0 %all-to-all-start = ((bf16[64,2,8,1536]{3,2,1,0:T(8,128)(2,1)}), bf16[64,2,8,1536]{3,2,1,0:T(8,128)(2,1)}, u32[]{:S(2)}, u32[]{:S(2)}) async-start(bf16[64,2,8,1536]{3,2,1,0:T(8,128)(2,1)} %bitcast.169), calls=%async_computation | async-start | bytes 6291456 | tf_op jit(solution)/shard_map/all_to_all | solution.py:142
  96.1 37.0 %all-gather.6.cloned.1.call-start = ((), (), s32[]{:S(2)}) async-start(), calls=%async_computation.9 | async-start | bytes 2621440 | tf_op jit(solution)/shard_map/all_gather | solution.py:114
  168.6 39.4 %all-to-all-start.3 = ((bf16[64,2,8,512]{3,2,1,0:T(8,128)(2,1)}), bf16[64,2,8,512]{3,2,1,0:T(8,128)(2,1)}, u32[]{:S(2)}, u32[]{:S(2)}) async-start(bf16[64,2,8,512]{3,2,1,0:T(8,128)(2,1)} %bitcast.38), calls=%async_computation.4 | async-start | bytes 2097152 | tf_op jit(solution)/shard_map/all_to_all | solution.py:150
  207.9 38.3 %all-to-all-start.2 = ((bf16[2,64,8,512]{3,2,0,1:T(8,128)(2,1)}), bf16[2,64,8,512]{3,2,0,1:T(8,128)(2,1)S(1)}, u32[]{:S(2)}, u32[]{:S(2)}) async-start(bf16[2,64,8,512]{3,2,0,1:T(8,128)(2,1)} %copy.78), calls=%async_computation.2 | async-start | bytes 2097152 | tf_op jit(solution)/shard_map/all_to_all | solution.py:148
  218.2 188.8 %reduce-scatter.3.cloned.1.call-start = ((), (), s32[]{:S(2)}) async-start(), calls=%async_computation.8 | async-start | bytes 5242880 | tf_op jit(solution)/shard_map/reduce_scatter | solution.py:161
  253.1 200.6 %reduce-scatter.5.cloned.1.call-start = ((), (), s32[]{:S(2)}) async-start(), calls=%async_computation.10 | async-start | bytes 5242880 | tf_op jit(solution)/shard_map/reduce_scatter | solution.py:177
  398.4 2.1 copy-start.3
  400.5 1.6 copy-start.5
  402.1 1.6 copy-start.6
  403.7 50.1 %copy-start.1 = (bf16[512,2048]{1,0:T(8,128)(2,1)S(1)}, bf16[512,2048]{1,0:T(8,128)(2,1)}, u32[]{:S(2)}) copy-start(bf16[512,2048]{1,0:T(8,128)(2,1)} %param.18) | copy-start | bytes 6291460
Sparse Core Ops, SparseCore 0:
  9.8 37.1 all-gather.3
  98.7 34.2 all-gather.5
  253.3 46.4 reduce-scatter.2
  407.1 46.6 reduce-scatter.4
where the time goes:
time: 466 us; the launch traced here: 461 us
  waiting for transfers between devices  137 us (29%)
  blocking collectives  124 us (27%)
  matrix products  83.9 us (18%)
  local copies, waits for them, and re-layouts  56.7 us (12%)
  starting transfers between devices  35.2 us (8%)
  between operations  14.3 us (3%)
  other arithmetic  8.37 us (2%)
    all_to_all x1, blocking collectives, body(): lax.all_to_all(from_owners(grad_slots), 'seq', split_axis=1, concat_axis=...  79.5 us
    reduce_scatter x1, waiting for transfers between devices, body(): lax.psum_scatter(partial_grad, 'tp', scatter_dimension=1, tiled=True)  44.7 us
    all_gather x1, blocking collectives, entering(): everything = lax.all_gather(x, axis)  44.2 us
    all_gather x1, waiting for transfers between devices, body(): lax.all_gather(grad_out, 'tp', axis=1, tiled=True)  36.1 us
    all_to_all x1, waiting for transfers between devices, body(): lax.all_to_all(to_owners(packed_rows), 'seq', split_axis=0, concat_axis=2...  29.1 us
    all_to_all x1, waiting for transfers between devices, body(): lax.all_to_all(from_owners(mixed_slots), 'seq', split_axis=1, concat_axis...  25.6 us
    sub x4, matrix products, cluster_probs(): raised = jnp.exp(scores - row_top)  16.6 us
    dot_general x2, matrix products, attention_core(): jnp.einsum('hqk,khd->qhd', grad_scores, key_rows, preferred_element_type=...  15.7 us
  transfers between devices with their start and end apart: 8, of which 4 were waited for; matrix products, arithmetic and copies ran while one was open for 31% of the time, Pallas kernels for 0%

commit v1 on v0

v1 whole, which is shorter than its diff:
```python
import jax
import jax.numpy as jnp
from jax import lax
from jax.sharding import PartitionSpec as P

HEAD_DIM = 128
CLUSTERS = 128
CAP = 256
MOST = 8
EMPTY = 128.0


def attention(query, key_rows, value_rows, grad_rows, usable):
    groups, rows, width = query.shape
    scale = HEAD_DIM ** (-0.5)

    def heads(x):
        return x.reshape(groups, rows, width // HEAD_DIM, HEAD_DIM)

    def product(spec, a, b):
        return jnp.einsum(spec, a, b, preferred_element_type=jnp.float32)

    query, key_rows, value_rows, grad_rows = (
        heads(query),
        heads(key_rows),
        heads(value_rows),
        heads(grad_rows),
    )
    scores = product("cqhd,ckhd->chqk", query, key_rows) * scale
    scores = jnp.where(usable[:, None, None, :], scores, -1e30)
    raised = jnp.exp(scores - jnp.max(scores, axis=-1, keepdims=True))
    probs = raised / jnp.sum(raised, axis=-1, keepdims=True)
    rounded = probs.astype(jnp.bfloat16)
    mixed = product("chqk,ckhd->cqhd", rounded, value_rows)
    grad_value = product("chqk,cqhd->ckhd", rounded, grad_rows)
    grad_probs = product("cqhd,ckhd->chqk", grad_rows, value_rows)
    inner = jnp.sum(grad_probs * probs, axis=-1, keepdims=True)
    grad_scores = (probs * (grad_probs - inner) * scale).astype(jnp.bfloat16)
    grad_query = product("chqk,ckhd->cqhd", grad_scores, key_rows)
    grad_key = product("chqk,cqhd->ckhd", grad_scores, query)

    def flat(x):
        return x.astype(jnp.bfloat16).reshape(groups * rows, width)

    return flat(mixed), flat(grad_query), flat(grad_key), flat(grad_value)


def body(normed, cluster, w_query, w_key, w_value, w_out, grad_out):
    seq_count = lax.axis_size("seq")
    tp_count = lax.axis_size("tp")
    here = CLUSTERS // seq_count
    tokens, width = normed.shape
    ids = cluster[:, 0]
    order = jnp.arange(tokens, dtype=jnp.int32)
    same = (ids[:, None] == ids[None, :]) & (order[None, :] < order[:, None])
    rank = jnp.sum(same.astype(jnp.int32), axis=1)
    slot = ids * MOST + rank
    places = jnp.arange(CLUSTERS * MOST, dtype=jnp.int32)
    spread = (places[:, None] == slot[None, :]).astype(jnp.bfloat16)
    both = jnp.concatenate([normed, grad_out], axis=1)
    packed = jnp.dot(spread, both, preferred_element_type=jnp.float32)
    filled = jnp.sum(spread.astype(jnp.float32), axis=1, keepdims=True)
    first = (jnp.arange(2 * width) == 0).astype(jnp.float32)
    packed = (packed + (1.0 - filled) * first[None, :] * EMPTY).astype(jnp.bfloat16)
    packed = packed.reshape(seq_count, here, MOST, 2 * width)
    arrived = lax.all_to_all(packed, "seq", split_axis=0, concat_axis=0, tiled=True)
    arrived = jnp.swapaxes(arrived, 0, 1).reshape(here, seq_count * MOST, 2 * width)
    valid = arrived[:, :, 0].astype(jnp.float32) < 0.5 * EMPTY
    slots = seq_count * MOST
    index = jnp.arange(slots)
    before = (index[:, None] < index[None, :]).astype(jnp.bfloat16)
    place = jnp.dot(valid.astype(jnp.bfloat16), before, preferred_element_type=jnp.float32)
    rows = jnp.arange(CAP, dtype=jnp.float32)
    choose = (
        (place[:, None, :] == rows[None, :, None]) & valid[:, None, :]
    ).astype(jnp.bfloat16)
    usable = jnp.sum(choose.astype(jnp.float32), axis=2) > 0.5
    compact = jnp.einsum(
        "crs,csf->crf", choose, arrived, preferred_element_type=jnp.float32
    ).astype(jnp.bfloat16)
    compact = compact.reshape(here * CAP, 2 * width)
    gathered = lax.all_gather(compact, "tp", axis=0)
    x = jnp.swapaxes(gathered[:, :, :width], 0, 1).reshape(here * CAP, tp_count * width)
    dy = jnp.swapaxes(gathered[:, :, width:], 0, 1).reshape(here * CAP, tp_count * width)

    def project(w):
        y = jnp.dot(x, w, preferred_element_type=jnp.float32).astype(jnp.bfloat16)
        return y.reshape(here, CAP, w.shape[1])

    contract = (((1,), (1,)), ((), ()))
    head_grads = (
        lax.dot_general(dy, w_out, contract, preferred_element_type=jnp.float32)
        .astype(jnp.bfloat16)
        .reshape(here, CAP, w_out.shape[0])
    )
    mixed, grad_query, grad_key, grad_value = attention(
        project(w_query), project(w_key), project(w_value), head_grads, usable
    )
    out_part = jnp.dot(mixed, w_out, preferred_element_type=jnp.float32)
    grad_part = (
        lax.dot_general(grad_query, w_query, contract, preferred_element_type=jnp.float32)
        + lax.dot_general(grad_key, w_key, contract, preferred_element_type=jnp.float32)
        + lax.dot_general(grad_value, w_value, contract, preferred_element_type=jnp.float32)
    )

    def pieces(part):
        return part.astype(jnp.bfloat16).reshape(here * CAP, tp_count, width)

    parts = jnp.concatenate([pieces(out_part), pieces(grad_part)], axis=2)
    parts = jnp.swapaxes(parts, 0, 1)
    parts = lax.all_to_all(parts, "tp", split_axis=0, concat_axis=0, tiled=True)
    mine = jnp.sum(parts.astype(jnp.float32), axis=0).astype(jnp.bfloat16)
    mine = mine.reshape(here, CAP, 2 * width)
    back = jnp.einsum(
        "crs,crf->scf", choose, mine, preferred_element_type=jnp.float32
    ).astype(jnp.bfloat16)
    back = jnp.swapaxes(back.reshape(seq_count, MOST, here, 2 * width), 1, 2)
    back = lax.all_to_all(back, "seq", split_axis=0, concat_axis=0, tiled=True)
    back = back.reshape(CLUSTERS * MOST, 2 * width)
    result = lax.dot_general(
        spread, back, (((0,), (0,)), ((), ())), preferred_element_type=jnp.float32
    )
    return (result[:, :width].astype(jnp.bfloat16), result[:, width:])


def solution(mesh):
    in_specs = (
        P("seq", "tp"),
        P("seq", None),
        P(None, "tp"),
        P(None, "tp"),
        P(None, "tp"),
        P("tp", None),
        P("seq", "tp"),
    )
    out_specs = (P("seq", "tp"), P("seq", "tp"))
    return jax.shard_map(body, mesh=mesh, in_specs=in_specs, out_specs=out_specs, check_vma=False)
```

time: 466 us -> 316 us (0.68)
  waiting for transfers between devices: 137 us -> 48.3 us
  blocking collectives: 124 us -> 175 us
  matrix products: 83.9 us -> 44 us
  starting transfers between devices: 35.2 us -> 0.04 us
  local copies, waits for them, and re-layouts: 56.7 us -> 26.5 us
    all_to_all x1 -> x3, blocking collectives: 79.5 us -> 175 us  [the longest x1 62.6 us: body(): lax.all_to_all(packed, 'seq', split_axis=0, concat_axis=0, tiled=True)]
    all_to_all x4 -> x0, waiting for transfers between devices: 54.8 us -> none  [the longest x1 29.1 us: body(): lax.all_to_all(to_owners(packed_rows), 'seq', split_axis=0, concat_axis=2...]
    reduce_scatter x2 -> x0, waiting for transfers between devices: 44.7 us -> none  [the longest x1 44.7 us: body(): lax.psum_scatter(partial_grad, 'tp', scatter_dimension=1, tiled=True)]
    all_gather x1 -> x0, blocking collectives: 44.2 us -> none  [entering(): everything = lax.all_gather(x, axis)]
    all_to_all x4 -> x0, starting transfers between devices: 34.6 us -> none  [the longest x1 10.5 us: body(): lax.all_to_all(to_owners(packed_rows), 'seq', split_axis=0, concat_axis=2...]
    dot_general x18, matrix products: 67.3 us -> 41.8 us  [the longest x5 17.4 us: product(): return jnp.einsum(spec, a, b, preferred_element_type=jnp.float32)]
    sub x4 -> x1, matrix products: 16.6 us -> 2.18 us  [attention(): raised = jnp.exp(scores - jnp.max(scores, axis=-1, keepdims=True))]
    scatter x3 -> x0, local copies, waits for them, and re-layouts: 13.2 us -> none  [the longest x2 9.47 us: to_owners(): jnp.zeros((CLUSTERS * MOST, rows.shape[1]), rows.dtype).at[slot_index]]
  transfers between devices with their start and end apart: 8 -> 1, of which waited for: 4 -> 1; matrix products, arithmetic and copies ran while one was open for 31% -> 0% of each run, Pallas kernels for 0% -> 0%
where the time goes in v1:
time: 316 us; the launch traced here: 315 us
  blocking collectives  175 us (55%)
  waiting for transfers between devices  48.3 us (15%)
  matrix products  44 us (14%)
  local copies, waits for them, and re-layouts  26.5 us (8%)
  between operations  14.3 us (5%)
  other arithmetic  6.79 us (2%)
    all_to_all x1, blocking collectives, body(): lax.all_to_all(packed, 'seq', split_axis=0, concat_axis=0, tiled=True)  62.6 us
    all_to_all x1, blocking collectives, body(): back = lax.all_to_all(back, 'seq', split_axis=0, concat_axis=0, tiled=True)  61.3 us
    all_to_all x1, blocking collectives, body(): parts = lax.all_to_all(parts, 'tp', split_axis=0, concat_axis=0, tiled=True)  51.3 us
    all_gather x1, waiting for transfers between devices, body(): gathered = lax.all_gather(compact, 'tp', axis=0)  48.2 us
    dot_general x5, matrix products, product(): return jnp.einsum(spec, a, b, preferred_element_type=jnp.float32)  17.4 us
    unnamed x30, local copies, waits for them, and re-layouts  9.01 us
    dot_general x3, matrix products, project(): y = jnp.dot(x, w, preferred_element_type=jnp.float32).astype(jnp.bfloat16)  8.39 us
  transfers between devices with their start and end apart: 1, of which 1 were waited for; matrix products, arithmetic and copies ran while one was open for 0% of the time, Pallas kernels for 0%

profile of v1, /device:TPU:1, one launch (start us, length us, event | category | flops | bytes accessed | tf_op | source)
XLA Modules:
  0.0 315.1 jit_solution(11808910619287864600)
XLA Ops:
  7.2 1.1 convert_reduce_fusion.2
  9.3 2.5 add_convert_fusion.1
  11.9 62.6 %all_to_all.15 = bf16[64,2,8,1024]{3,2,1,0:T(8,128)(2,1)S(1)} all-to-all(bf16[64,2,8,1024]{3,2,1,0:T(8,128)(2,1)S(1)} %bitcast.93), channel_id=1, replica_groups=mesh['seq'=64,'tp'=4] {'seq'}, dimensions={0} | all-to-all | bytes 4194304 | tf_op jit(solution)/shard_map/all_to_all | solution.py:66
  75.1 2.1 convolution_convert_fusion.1
  77.6 48.2 %all-gather.2.cloned.1.call-done = bf16[4,512,1024]{2,1,0:T(8,128)(2,1)} async-done(((bf16[1,512,1024]{2,1,0:T(8,128)(2,1)}), bf16[4,512,1024]{2,1,0:T(8,128)(2,1)}) %all-gather.2.cloned.1.call-update) | async-done | bytes 4194320 | tf_op jit(solution)/shard_map/all_gather | solution.py:82
  125.8 4.5 %fusion.74 = (bf16[4,512,512]{2,1,0:T(8,128)(2,1)}, bf16[4,512,512]{2,1,0:T(8,128)(2,1)}) fusion(bf16[4,512,1024]{2,1,0:T(8,128)(2,1)} %all-gather.2.cloned.1.call-done), kind=kLoop, calls=%fused_computation.91 | loop fusion | bytes 8388608 | tf_op jit(solution)/shard_map/slice | solution.py:84
  130.3 4.1 %copy.95 = bf16[4,512,512]{1,2,0:T(8,128)(2,1)} copy(bf16[4,512,512]{2,1,0:T(8,128)(2,1)} %get-tuple-element.2) | data formatting | bytes 4194304
  134.4 2.9 convolution_convert_fusion.2
  137.5 1.1 copy.83
  138.5 4.1 %copy.94 = bf16[4,512,512]{1,2,0:T(8,128)(2,1)} copy(bf16[4,512,512]{2,1,0:T(8,128)(2,1)} %get-tuple-element.3) | data formatting | bytes 4194304
  142.7 3.5 %convolution_convert_fusion.3 = bf16[512,512]{1,0:T(8,128)(2,1)S(1)} fusion(bf16[512,2048]{0,1:T(8,128)(2,1)} %bitcast.84, bf16[2048,512]{1,0:T(8,128)(2,1)} %param.10), kind=kOutput, calls=%fused_computation.27 | convolution fusion | flops 1074003968 | bytes 4718592 | tf_op jit(solution)/shard_map/dot_general | solution.py:87
  147.4 3.6 %convolution_convert_fusion.4 = bf16[512,512]{1,0:T(8,128)(2,1)S(1)} fusion(bf16[512,2048]{0,1:T(8,128)(2,1)} %bitcast.85, bf16[2048,512]{1,0:T(8,128)(2,1)} %param.9), kind=kOutput, calls=%fused_computation.28 | convolution fusion | flops 1074003968 | bytes 4718592 | tf_op jit(solution)/shard_map/dot_general | solution.py:87
  151.0 1.3 convolution_convert_fusion.5
  153.4 1.1 copy.80
  154.5 3.0 fusion.62
  157.5 2.2 fusion.75
  159.7 5.0 %fusion.25 = bf16[2,256,4,128]{1,3,2,0:T(8,128)(2,1)} fusion(bf16[2,256,4,128]{1,3,2,0:T(8,128)(2,1)S(1)} %copy-done.10, f32[2,4,256,256]{2,3,1,0:T(8,128)} %fusion.62, f32[2,4,256,256]{2,3,1,0:T(8,128)} %get-tuple-element.5, f32[2,4,256]{2,1,0:T(4,128)S(1)} %get-tuple-element.4), kind=kOutput, calls=%fused_computation.35 | convolution fusion | flops 138152192 | bytes 5251072 | tf_op jit(solution)/shard_map/chqk,ckhd->cqhd/dot_general | solution.py:21
  164.7 5.1 %fusion.22 = bf16[2,256,4,128]{1,3,2,0:T(8,128)(2,1)} fusion(bf16[2,256,4,128]{1,3,2,0:T(8,128)(2,1)S(1)} %copy-done.11, f32[2,4,256,256]{2,3,1,0:T(8,128)} %fusion.62, f32[2,4,256,256]{2,3,1,0:T(8,128)} %get-tuple-element.5, f32[2,4,256]{2,1,0:T(4,128)S(1)} %get-tuple-element.4), kind=kOutput, calls=%fused_computation.34 | convolution fusion | flops 138152192 | bytes 5251072 | tf_op jit(solution)/shard_map/chqk,cqhd->ckhd/dot_general | solution.py:21
  169.8 3.0 fusion.21
  172.9 1.2 fusion.20
  174.3 1.3 copy.79
  175.6 2.1 copy.73
  177.7 2.1 copy.85
  179.8 2.4 convolution_convert_fusion
  182.3 1.3 fusion.49
  183.9 1.3 fusion.46
  185.5 1.3 add_convert_fusion
  188.1 51.3 %all_to_all.16 = bf16[4,512,1024]{2,1,0:T(8,128)(2,1)} all-to-all(bf16[4,512,1024]{2,1,0:T(8,128)(2,1)S(1)} %maximum_bitcast_fusion), channel_id=1, replica_groups=mesh['seq'=64,'tp'=4] {'tp'}, dimensions={0} | all-to-all | bytes 8388608 | tf_op jit(solution)/shard_map/all_to_all | solution.py:111
  239.4 3.3 %reduce_sum.62 = bf16[512,1024]{1,0:T(8,128)(2,1)S(1)} reduce(bf16[4,512,1024]{2,1,0:T(8,128)(2,1)} %all_to_all.16, bf16[]{:T(256)} %constant.22.clone.1), dimensions={0}, to_apply=%region_6.7 | reduce | flops 1572864 | bytes 5242882 | tf_op jit(solution)/shard_map/reduce_sum | solution.py:112
  243.7 61.3 %all_to_all.17 = bf16[64,2,8,1024]{3,2,1,0:T(8,128)(2,1)S(1)} all-to-all(bf16[64,2,8,1024]{3,2,1,0:T(8,128)(2,1)S(1)} %bitcast.88), channel_id=1, replica_groups=mesh['seq'=64,'tp'=4] {'seq'}, dimensions={0} | all-to-all | bytes 4194304 | tf_op jit(solution)/shard_map/all_to_all | solution.py:118
  305.0 1.3 fusion.3
  307.2 1.1 slice.25
  (50 shorter events, 8.4 us)
Async XLA Ops:
  7.2 127.3 %copy-start = (bf16[512,2048]{1,0:T(8,128)(2,1)S(1)}, bf16[512,2048]{1,0:T(8,128)(2,1)}, u32[]{:S(2)}) copy-start(bf16[512,2048]{1,0:T(8,128)(2,1)} %param.12) | copy-start | bytes 6291460
  7.2 118.6 %all-gather.2.cloned.1.call-start = ((), (), s32[]{:S(2)}) async-start(), calls=%async_computation.3 | async-start | bytes 5242880 | tf_op jit(solution)/shard_map/all_gather | solution.py:82
  147.4 3.6 %copy-start.2 = (bf16[4,512,512]{1,2,0:T(8,128)(2,1)S(1)}, bf16[4,512,512]{1,2,0:T(8,128)(2,1)}, u32[]{:S(2)}) copy-start(bf16[4,512,512]{1,2,0:T(8,128)(2,1)} %copy.94) | copy-start | bytes 6291460
  147.4 3.7 %copy-start.3 = (bf16[2048,512]{1,0:T(8,128)(2,1)S(1)}, bf16[2048,512]{1,0:T(8,128)(2,1)}, u32[]{:S(2)}) copy-start(bf16[2048,512]{1,0:T(8,128)(2,1)} %param.11) | copy-start | bytes 6291460
  153.4 4.1 %copy-start.10 = (bf16[2,256,4,128]{1,3,2,0:T(8,128)(2,1)S(1)}, bf16[2,256,4,128]{1,3,2,0:T(8,128)(2,1)}, u32[]{:S(2)}) copy-start(bf16[2,256,4,128]{1,3,2,0:T(8,128)(2,1)} %copy.77) | copy-start | bytes 1572868
  154.4 3.0 copy-start.11
  164.7 5.1 %copy-start.8 = (bf16[2,256,4,128]{1,3,2,0:T(8,128)(2,1)S(1)}, bf16[2,256,4,128]{1,3,2,0:T(8,128)(2,1)}, u32[]{:S(2)}) copy-start(bf16[2,256,4,128]{1,3,2,0:T(8,128)(2,1)} %copy.83) | copy-start | bytes 1572868
  169.8 3.0 copy-start.9
  169.8 3.0 copy-start.13
  172.9 1.2 copy-start.12
  179.8 2.5 copy-start.5
  182.3 1.6 copy-start.6
  183.9 1.6 copy-start.4
  183.9 1.7 copy-start.7
  305.0 3.3 %copy-start.1 = (bf16[512,2048]{1,0:T(8,128)(2,1)S(1)}, bf16[512,2048]{1,0:T(8,128)(2,1)}, u32[]{:S(2)}) copy-start(bf16[512,2048]{1,0:T(8,128)(2,1)} %param.12) | copy-start | bytes 6291460
Sparse Core Ops, SparseCore 0:
  77.3 48.4 all-gather.1

commit v2 on v1

v2 whole, which is shorter than its diff:
```python
import functools

import jax
import jax.numpy as jnp
from jax import lax
from jax.experimental import pallas as pl
from jax.experimental.pallas import tpu as pltpu
from jax.sharding import PartitionSpec as P

MESH = pl.DeviceIdType.MESH
HEAD_DIM = 128
CLUSTERS = 128
CAP = 256
MOST = 8
EMPTY = 128.0
PAIR = 2 * MOST
STRIDE = 27
F32 = jnp.float32
BF16 = jnp.bfloat16


def product(a, b, contract=(1, 0)):
    dims = (((contract[0],), (contract[1],)), ((), ()))
    return lax.dot_general(a, b, dims, preferred_element_type=F32)


def iota(shape, dim):
    return lax.broadcasted_iota(jnp.int32, shape, dim)


def kernel(
    peers,
    ring,
    ids_row,
    ids_col,
    normed,
    grad_out,
    wq_hbm,
    wk_hbm,
    wv_hbm,
    wo_hbm,
    attended,
    grad_normed,
    wq,
    wk,
    wv,
    wo,
    packed,
    recv,
    expanded,
    back,
    xin,
    sums_out,
    sums_in,
    before,
    choose,
    count,
    heads,
    own,
    w_sem,
    go_send,
    go_recv,
    back_send,
    back_recv,
    x_send,
    x_recv,
    r_send,
    r_recv,
):
    s, t = lax.axis_index("seq"), lax.axis_index("tp")
    right, left, across = lax.rem(t + 1, ring), lax.rem(t + ring - 1, ring), lax.rem(t + 2, ring)
    tokens, width = normed.shape
    slots = peers * PAIR
    tile = 256

    weights = [
        pltpu.make_async_copy(src, dst, w_sem.at[i])
        for i, (src, dst) in enumerate(
            ((wq_hbm, wq), (wk_hbm, wk), (wv_hbm, wv), (wo_hbm, wo))
        )
    ]
    for copy in weights:
        copy.start()

    barrier = pltpu.get_barrier_semaphore()

    @pl.loop(1, peers)
    def _(r):
        pl.semaphore_signal(
            barrier, inc=1, device_id=(lax.rem(s + r, peers), t), device_id_type=MESH
        )

    for d in range(1, ring):
        pl.semaphore_signal(
            barrier, inc=1, device_id=(s, lax.rem(t + d, ring)), device_id_type=MESH
        )

    same = ids_col[...] == ids_row[...]
    above = iota((tokens, tokens), 0) < iota((tokens, tokens), 1)
    below = iota((tokens, tokens), 0) > iota((tokens, tokens), 1)
    rank_row = jnp.sum(jnp.where(same & above, 1.0, 0.0), axis=0, keepdims=True)
    rank_col = jnp.sum(jnp.where(same & below, 1.0, 0.0), axis=1, keepdims=True)

    def place(ids, rank):
        return ((ids & 1) * peers + (ids >> 1)) * PAIR + rank.astype(jnp.int32)

    place_row = place(ids_row[...], rank_row)
    place_col = place(ids_col[...], rank_col)

    def pack(half):
        @pl.loop(0, slots // tile)
        def _(i):
            row = iota((tile, tokens), 0) + (half * slots + i * tile)
            put = (row == place_row).astype(F32)
            put_grad = (row == place_row + MOST).astype(BF16)
            filled = jnp.sum(put, axis=1, keepdims=True)
            rows = product(put.astype(BF16), normed[...]) + product(put_grad, grad_out[...])
            lane = iota((tile, width), 1)
            odd = lax.rem(iota((tile, width), 0), PAIR)
            mark = (odd < MOST) & (lane < 128) & (filled < 0.5)
            rows = jnp.where(mark, EMPTY, rows).astype(BF16)
            packed[half, pl.ds(i * (tile // PAIR), tile // PAIR)] = rows.reshape(
                tile // PAIR, PAIR, width
            )

    def send_all(half, src, dst, send_sem, recv_sem):
        pltpu.make_async_copy(src.at[half, s], dst.at[half, s], recv_sem.at[half]).start()

        @pl.loop(1, peers)
        def _(r):
            peer = lax.rem(s + r * STRIDE, peers)
            pltpu.make_async_remote_copy(
                src_ref=src.at[half, peer],
                dst_ref=dst.at[half, s],
                send_sem=send_sem.at[half],
                recv_sem=recv_sem.at[half],
                device_id=(peer, t),
                device_id_type=MESH,
            ).start()

    def wait_all(half, dst, recv_sem):
        pltpu.make_async_copy(dst.at[half], dst.at[half], recv_sem.at[half]).wait()

    def wait_sent(half, src, send_sem):
        part = src.at[half, pl.ds(0, peers - 1)]
        pltpu.make_async_copy(part, part, send_sem.at[half]).wait()

    def hop(src, dst, send_sem, recv_sem, target):
        return pltpu.make_async_remote_copy(
            src_ref=src,
            dst_ref=dst,
            send_sem=send_sem,
            recv_sem=recv_sem,
            device_id=(s, target),
            device_id_type=MESH,
        )

    def gather_hops(half):
        def one(i, src, dst, target):
            return hop(src, dst, x_send.at[half, i], x_recv.at[half, i], target)

        return (
            one(0, xin.at[half, 0], xin.at[half, 1], right),
            one(1, xin.at[half, 0], xin.at[half, 2], left),
            one(2, xin.at[half, 1, 0], xin.at[half, 3, 0], right),
            one(3, xin.at[half, 2, 1], xin.at[half, 3, 1], left),
        )

    def sum_hops(half):
        targets = (right, left, right, left, right, left)
        return [
            hop(
                sums_out.at[half, i],
                sums_in.at[half, i],
                r_send.at[half, i],
                r_recv.at[half, i],
                target,
            )
            for i, target in enumerate(targets)
        ]

    def compact(half):
        wait_all(half, recv, go_recv)
        first = recv[half, :, :, :128].astype(F32)
        valid = (first[:, :MOST] < 0.5 * EMPTY).astype(F32)
        zero = jnp.zeros_like(valid)
        only = jnp.concatenate([valid, zero], axis=1).reshape(slots, 128)
        valid = jnp.concatenate([valid, valid], axis=1).reshape(slots, 128)
        rank = product(before[...], only.astype(BF16))
        count[half] = jnp.broadcast_to(jnp.sum(only, axis=0, keepdims=True), (8, 128))
        second = lax.rem(iota((slots, 128), 0), PAIR) >= MOST
        kept = (valid > 0.5) & (rank < CAP)
        goal = jnp.where(kept, rank + jnp.where(second, CAP * 1.0, 0.0), -1.0).astype(jnp.int32)
        for k in range(2 * CAP // 128):
            choose[half, :, k * 128 : (k + 1) * 128] = (
                goal == iota((slots, 128), 1) + k * 128
            ).astype(BF16)
        rows = recv[half].reshape(slots, width)
        both = product(choose[half], rows, (0, 0)).astype(BF16)
        xin[half, 0] = both.reshape(2, CAP, width)
        hops = gather_hops(half)
        hops[0].start()
        hops[1].start()

    def relay(half):
        hops = gather_hops(half)
        hops[0].wait_recv()
        hops[2].start()
        hops[1].wait_recv()
        hops[3].start()

    def project(half):
        hops = gather_hops(half)
        hops[2].wait_recv()
        hops[3].wait_recv()
        order = (t, left, right, across)
        for i, w in enumerate((wq, wk, wv)):
            total = None
            for k in range(4):
                part = product(xin[half, k, 0], w[pl.ds(order[k] * width, width), :])
                total = part if total is None else total + part
            heads[i] = total.astype(BF16)
        total = None
        for k in range(4):
            columns = pl.ds(pl.multiple_of(order[k] * width, width), width)
            part = product(xin[half, k, 1], wo[:, columns], (1, 1))
            total = part if total is None else total + part
        heads[3] = total.astype(BF16)

    def attend(half):
        scale = HEAD_DIM ** (-0.5)
        usable = count[half, :1, :1] > iota((1, CAP), 1).astype(F32)

        @pl.loop(0, width // HEAD_DIM)
        def _(h):
            at = pl.ds(pl.multiple_of(h * HEAD_DIM, HEAD_DIM), HEAD_DIM)
            query, key_rows, value_rows, grad_rows = (heads[i, :, at] for i in range(4))
            scores = product(query, key_rows, (1, 1)) * scale
            scores = jnp.where(usable, scores, -1e30)
            raised = jnp.exp(scores - jnp.max(scores, axis=1, keepdims=True))
            probs = raised / jnp.sum(raised, axis=1, keepdims=True)
            rounded = probs.astype(BF16)
            grad_probs = product(grad_rows, value_rows, (1, 1))
            inner = jnp.sum(grad_probs * probs, axis=1, keepdims=True)
            grad_scores = (probs * (grad_probs - inner) * scale).astype(BF16)
            heads[4, :, at] = product(rounded, value_rows).astype(BF16)
            heads[5, :, at] = product(grad_scores, key_rows).astype(BF16)
            heads[6, :, at] = product(grad_scores, query, (0, 0)).astype(BF16)
            heads[7, :, at] = product(rounded, grad_rows, (0, 0)).astype(BF16)

    def out_part(target):
        columns = pl.ds(pl.multiple_of(target * width, width), width)
        return product(heads[4], wo[:, columns])

    def grad_part(target):
        rows = pl.ds(target * width, width)
        return (
            product(heads[5], wq[rows, :], (1, 1))
            + product(heads[6], wk[rows, :], (1, 1))
            + product(heads[7], wv[rows, :], (1, 1))
        )

    def outputs(half):
        hops = sum_hops(half)
        for i, part in ((0, out_part(across)), (1, grad_part(across)), (4, grad_part(right)), (5, out_part(left))):
            sums_out[half, i] = part.astype(BF16)
            hops[i].start()
        own[half, 0] = out_part(t)
        own[half, 1] = grad_part(t)
        for i, part in ((2, out_part(right)), (3, grad_part(left))):
            hops[i - 2].wait_recv()
            sums_out[half, i] = (part + sums_in[half, i - 2].astype(F32)).astype(BF16)
            hops[i].start()

    def finish(half):
        hops = sum_hops(half)
        for i in range(2, 6):
            hops[i].wait_recv()
        out = own[half, 0] + sums_in[half, 2].astype(F32) + sums_in[half, 5].astype(F32)
        grad = own[half, 1] + sums_in[half, 3].astype(F32) + sums_in[half, 4].astype(F32)
        both = jnp.concatenate([out.astype(BF16), grad.astype(BF16)], axis=0)

        @pl.loop(0, slots // tile)
        def _(i):
            rows = product(choose[half, pl.ds(i * tile, tile), :], both).astype(BF16)
            expanded[half, pl.ds(i * (tile // PAIR), tile // PAIR)] = rows.reshape(
                tile // PAIR, PAIR, width
            )

        send_all(half, expanded, back, back_send, back_recv)

    def unpack(half):
        wait_all(half, back, back_recv)
        rows = back[half].reshape(slots, width)
        lane = iota((tokens, slots), 1) + half * slots
        out = product((lane == place_col).astype(BF16), rows)
        grad = product((lane == place_col + MOST).astype(BF16), rows)
        if half == 0:
            attended[...] = out.astype(BF16)
            grad_normed[...] = grad
        else:
            attended[...] = (attended[...].astype(F32) + out).astype(BF16)
            grad_normed[...] = grad_normed[...] + grad

    pack(0)
    pl.semaphore_wait(barrier, peers - 1 + ring - 1)
    send_all(0, packed, recv, go_send, go_recv)
    pack(1)
    send_all(1, packed, recv, go_send, go_recv)

    @pl.loop(0, slots // tile)
    def _(i):
        row, column = iota((tile, slots), 0) + i * tile, iota((tile, slots), 1)
        number = (row >> 4) * MOST + (row & (MOST - 1))
        other = (column >> 4) * MOST + (column & (MOST - 1))
        before[pl.ds(i * tile, tile), :] = (other < number).astype(BF16)

    for copy in weights:
        copy.wait()
    compact(0)
    relay(0)
    project(0)
    attend(0)
    compact(1)
    outputs(0)
    relay(1)
    finish(0)
    project(1)
    attend(1)
    outputs(1)
    finish(1)
    unpack(0)
    unpack(1)

    for half in range(2):
        wait_sent(half, packed, go_send)
        wait_sent(half, expanded, back_send)
        for copy in gather_hops(half):
            copy.wait_send()
        for copy in sum_hops(half):
            copy.wait_send()


def body(normed, cluster, w_query, w_key, w_value, w_out, grad_out):
    peers, ring = lax.axis_size("seq"), lax.axis_size("tp")
    tokens, width = normed.shape
    slots = peers * PAIR
    vmem = pl.BlockSpec(memory_space=pltpu.VMEM)
    anywhere = pl.BlockSpec(memory_space=pl.ANY)
    dma = pltpu.SemaphoreType.DMA
    return pl.pallas_call(
        functools.partial(kernel, peers, ring),
        out_shape=(
            jax.ShapeDtypeStruct((tokens, width), BF16),
            jax.ShapeDtypeStruct((tokens, width), F32),
        ),
        in_specs=[vmem] * 4 + [anywhere] * 4,
        out_specs=(vmem, vmem),
        scratch_shapes=[
            pltpu.VMEM(w_query.shape, BF16),
            pltpu.VMEM(w_key.shape, BF16),
            pltpu.VMEM(w_value.shape, BF16),
            pltpu.VMEM(w_out.shape, BF16),
            pltpu.VMEM((2, peers, PAIR, width), BF16),
            pltpu.VMEM((2, peers, PAIR, width), BF16),
            pltpu.VMEM((2, peers, PAIR, width), BF16),
            pltpu.VMEM((2, peers, PAIR, width), BF16),
            pltpu.VMEM((2, ring, 2, CAP, width), BF16),
            pltpu.VMEM((2, 6, CAP, width), BF16),
            pltpu.VMEM((2, 6, CAP, width), BF16),
            pltpu.VMEM((slots, slots), BF16),
            pltpu.VMEM((2, slots, 2 * CAP), BF16),
            pltpu.VMEM((2, 8, 128), F32),
            pltpu.VMEM((8, CAP, width), BF16),
            pltpu.VMEM((2, 2, CAP, width), F32),
            dma((4,)),
            dma((2,)),
            dma((2,)),
            dma((2,)),
            dma((2,)),
            dma((2, 4)),
            dma((2, 4)),
            dma((2, 6)),
            dma((2, 6)),
        ],
        compiler_params=pltpu.CompilerParams(
            collective_id=0, has_side_effects=True, vmem_limit_bytes=60 * 2**20
        ),
        name="routed",
    )(cluster.reshape(1, tokens), cluster, normed, grad_out, w_query, w_key, w_value, w_out)


def solution(mesh):
    in_specs = (
        P("seq", "tp"),
        P("seq", None),
        P(None, "tp"),
        P(None, "tp"),
        P(None, "tp"),
        P("tp", None),
        P("seq", "tp"),
    )
    out_specs = (P("seq", "tp"), P("seq", "tp"))
    return jax.shard_map(body, mesh=mesh, in_specs=in_specs, out_specs=out_specs, check_vma=False)
```

time: 316 us -> 169 us (0.53)
  blocking collectives: 175 us -> 0 us
  Pallas kernels: 0 us -> 162 us
  waiting for transfers between devices: 48.3 us -> 0 us
  matrix products: 44 us -> 0 us
  local copies, waits for them, and re-layouts: 26.5 us -> 5.67 us
  between operations: 14.3 us -> 0.64 us
  other arithmetic: 6.79 us -> 0 us
    all_to_all x3 -> x0, blocking collectives: 175 us -> none  [the longest x1 62.6 us: body(): lax.all_to_all(packed, 'seq', split_axis=0, concat_axis=0, tiled=True)]
    pallas_call x0 -> x1, Pallas kernels: none -> 162 us  [body(): pl.pallas_call(functools.partial(kernel, peers, ring), out_shape=(jax.Sha...]
    all_gather x1 -> x0, waiting for transfers between devices: 48.2 us -> none  [body(): gathered = lax.all_gather(compact, 'tp', axis=0)]
    dot_general x18 -> x0, matrix products: 41.8 us -> none  [the longest x5 17.4 us: product(): return jnp.einsum(spec, a, b, preferred_element_type=jnp.float32)]
    slice x3 -> x0, local copies, waits for them, and re-layouts: 6.42 us -> none  [the longest x1 4.48 us: body(): gathered[:, :, width:]]
    convert_element_type x4 -> x0, local copies, waits for them, and re-layouts: 5.78 us -> none  [flat(): return x.astype(jnp.bfloat16).reshape(groups * rows, width)]
    reduce_sum x4 -> x0, other arithmetic: 5.05 us -> none  [the longest x1 3.32 us: body(): mine = jnp.sum(parts.astype(jnp.float32), axis=0).astype(jnp.bfloat16)]
    another operation x7 -> x0, local copies, waits for them, and re-layouts: 4.49 us -> none  [heads(): return x.reshape(groups, rows, width // HEAD_DIM, HEAD_DIM)]
  transfers between devices with their start and end apart: 1 -> 0, of which waited for: 1 -> 0; matrix products, arithmetic and copies ran while one was open for 0% -> 0% of each run, Pallas kernels for 0% -> 0%
where the time goes in v2:
time: 169 us
  Pallas kernels  162 us (96%)
  local copies, waits for them, and re-layouts  5.67 us (3%)
    pallas_call x1, Pallas kernels, body(): pl.pallas_call(functools.partial(kernel, peers, ring), out_shape=(jax.Sha...  162 us
    unnamed x3, local copies, waits for them, and re-layouts  5.67 us

profile of v2, /device:TPU:1, one launch (start us, length us, event | category | flops | bytes accessed | tf_op | source)
XLA Modules:
  0.0 168.6 jit_solution(5729550557385225646)
XLA Ops:
  0.6 1.5 copy.9.ids_col
  2.2 162.3 %routed.1 = (bf16[512,512]{1,0:T(8,128)(2,1)}, f32[512,512]{1,0:T(8,128)}) custom-call(s32[1,512]{1,0:T(1,128)} %bitcast.1, s32[512,1]{1,0:T(8,128)} %copy.9.ids_col, bf16[512,512]{1,0:T(8,128)(2,1)} %normed.1, bf16[512,512]{1,0:T(8,128)(2,1)} %grad_out.1, bf16[2048,512]{1,0:T(8,128)(2,1)} %wq_hbm.1, bf16[2048,512]{1,0:T(8,128)(2,1)} %wk_hbm.1, ...), custom_call_target="tpu_custom_call" | custom-call | tf_op jit(solution)/shard_map/routed/pallas_call | solution.py:351
  164.5 1.9 %copy.12 = bf16[512,512]{1,0:T(8,128)(2,1)} copy(bf16[512,512]{1,0:T(8,128)(2,1)} %get-tuple-element.4) | data formatting | bytes 1048576
  166.4 2.3 %copy.13 = f32[512,512]{1,0:T(8,128)} copy(f32[512,512]{1,0:T(8,128)} %get-tuple-element.5) | data formatting | bytes 2097152

commit v3 on v2

v3 whole, which is shorter than its diff:
```python
import functools

import jax
import jax.numpy as jnp
from jax import lax
from jax.experimental import pallas as pl
from jax.experimental.pallas import tpu as pltpu
from jax.sharding import PartitionSpec as P

MESH = pl.DeviceIdType.MESH
HEAD_DIM = 128
CLUSTERS = 128
CAP = 256
MOST = 8
EMPTY = 128.0
PAIR = 2 * MOST
STRIDE = 27
PARTS = 2
F32 = jnp.float32
BF16 = jnp.bfloat16


def product(a, b, contract=(1, 0)):
    dims = (((contract[0],), (contract[1],)), ((), ()))
    return lax.dot_general(a, b, dims, preferred_element_type=F32)


def iota(shape, dim):
    return lax.broadcasted_iota(jnp.int32, shape, dim)


def kernel(
    peers,
    ring,
    ids_row,
    normed,
    grad_out,
    wq_hbm,
    wk_hbm,
    wv_hbm,
    wo_hbm,
    attended,
    grad_normed,
    wq,
    wk,
    wv,
    wo,
    packed,
    recv,
    expanded,
    back,
    xin,
    sums_out,
    sums_in,
    before,
    choose,
    gather_rows,
    take,
    count,
    heads,
    total,
    own,
    w_sem,
    go_send,
    go_recv,
    back_send,
    back_recv,
    x_send,
    x_recv,
    r_send,
    r_recv,
):
    s, t = lax.axis_index("seq"), lax.axis_index("tp")
    right, left, across = lax.rem(t + 1, ring), lax.rem(t + ring - 1, ring), lax.rem(t + 2, ring)
    tokens, width = normed.shape
    part_width = width // PARTS
    slots = peers * PAIR
    tile = 256

    weights = [
        pltpu.make_async_copy(src, dst, w_sem.at[i])
        for i, (src, dst) in enumerate(
            ((wq_hbm, wq), (wk_hbm, wk), (wv_hbm, wv), (wo_hbm, wo))
        )
    ]
    for copy in weights:
        copy.start()

    barrier = pltpu.get_barrier_semaphore()

    @pl.loop(1, peers)
    def _(r):
        pl.semaphore_signal(
            barrier, inc=1, device_id=(lax.rem(s + r, peers), t), device_id_type=MESH
        )

    for d in range(1, ring):
        pl.semaphore_signal(
            barrier, inc=1, device_id=(s, lax.rem(t + d, ring)), device_id_type=MESH
        )

    def column(row):
        wide = jnp.broadcast_to(row.astype(F32), (128, tokens))
        blocks = [jnp.transpose(wide[:, i : i + 128]) for i in range(0, tokens, 128)]
        return jnp.concatenate(blocks, axis=0)[:, :1].astype(jnp.int32)

    same = column(ids_row[...]) == ids_row[...]
    above = iota((tokens, tokens), 0) < iota((tokens, tokens), 1)
    rank_row = jnp.sum(jnp.where(same & above, 1.0, 0.0), axis=0, keepdims=True)
    place_row = ((ids_row[...] & 1) * peers + (ids_row[...] >> 1)) * PAIR + rank_row.astype(
        jnp.int32
    )

    def pack(half):
        @pl.loop(0, slots // tile)
        def _(i):
            row = iota((tile, tokens), 0) + (half * slots + i * tile)
            put = (row == place_row).astype(F32)
            put_grad = (row == place_row + MOST).astype(BF16)
            filled = jnp.sum(put, axis=1, keepdims=True)
            rows = product(put.astype(BF16), normed[...]) + product(put_grad, grad_out[...])
            odd = lax.rem(iota((tile, 128), 0), PAIR)
            mark = (odd < MOST) & (filled < 0.5)
            first = jnp.where(mark, EMPTY, rows[:, :128])
            rows = jnp.concatenate([first, rows[:, 128:]], axis=1).astype(BF16)
            for part in range(PARTS):
                some = rows[:, part * part_width : (part + 1) * part_width]
                packed[half, part, pl.ds(i * (tile // PAIR), tile // PAIR)] = some.reshape(
                    tile // PAIR, PAIR, part_width
                )

    def send_all(half, part, src, dst, send_sem, recv_sem):
        pltpu.make_async_copy(
            src.at[half, part, s], dst.at[half, part, s], recv_sem.at[half, part]
        ).start()

        @pl.loop(1, peers)
        def _(r):
            peer = lax.rem(s + r * STRIDE, peers)
            pltpu.make_async_remote_copy(
                src_ref=src.at[half, part, peer],
                dst_ref=dst.at[half, part, s],
                send_sem=send_sem.at[half, part],
                recv_sem=recv_sem.at[half, part],
                device_id=(peer, t),
                device_id_type=MESH,
            ).start()

    def wait_all(half, part, dst, recv_sem):
        everything = dst.at[half, part]
        pltpu.make_async_copy(everything, everything, recv_sem.at[half, part]).wait()

    def wait_sent(half, part, src, send_sem):
        others = src.at[half, part, pl.ds(0, peers - 1)]
        pltpu.make_async_copy(others, others, send_sem.at[half, part]).wait()

    def hop(src, dst, send_sem, recv_sem, target):
        return pltpu.make_async_remote_copy(
            src_ref=src,
            dst_ref=dst,
            send_sem=send_sem,
            recv_sem=recv_sem,
            device_id=(s, target),
            device_id_type=MESH,
        )

    def gather_hop(half, part, i):
        block = xin.at[half, part]
        src, dst, target = (
            (block.at[0], block.at[1], right),
            (block.at[0], block.at[2], left),
            (block.at[1, 0], block.at[3, 0], right),
            (block.at[2, 1], block.at[3, 1], left),
        )[i]
        return hop(src, dst, x_send.at[half, part, i], x_recv.at[half, part, i], target)

    def sum_hop(half, part, i):
        return hop(
            sums_out.at[half, part, i],
            sums_in.at[half, part, i],
            r_send.at[half, part, i],
            r_recv.at[half, part, i],
            (right, left)[i % 2],
        )

    def rank_slots(half):
        first = recv[half, 0, :, :, :128].astype(F32)
        valid = (first[:, :MOST] < 0.5 * EMPTY).astype(F32)
        zero = jnp.zeros_like(valid)
        only = jnp.concatenate([valid, zero], axis=1).reshape(slots, 128)
        valid = jnp.concatenate([valid, valid], axis=1).reshape(slots, 128)
        rank = product(before[...], only.astype(BF16))
        count[half] = jnp.broadcast_to(jnp.sum(only, axis=0, keepdims=True), (8, 128))
        second = lax.rem(iota((slots, 128), 0), PAIR) >= MOST
        kept = (valid > 0.5) & (rank < CAP)
        goal = jnp.where(kept, rank + jnp.where(second, CAP * 1.0, 0.0), -1.0)
        blocks = [jnp.transpose(goal[i : i + 128]) for i in range(0, slots, 128)]
        goal_row = jnp.concatenate(blocks, axis=1)[:1].astype(jnp.int32)
        goal = goal.astype(jnp.int32)
        for k in range(0, 2 * CAP, 128):
            choose[half, :, k : k + 128] = (goal == iota((slots, 128), 1) + k).astype(BF16)
            gather_rows[half, k : k + 128] = (goal_row == iota((128, slots), 0) + k).astype(BF16)

    def compact(half, part):
        wait_all(half, part, recv, go_recv)
        if part == 0:
            rank_slots(half)
        rows = recv[half, part].reshape(slots, part_width)
        both = product(gather_rows[half], rows).astype(BF16)
        xin[half, part, 0] = both.reshape(2, CAP, part_width)
        gather_hop(half, part, 0).start()
        gather_hop(half, part, 1).start()

    def relay(half, part):
        gather_hop(half, part, 0).wait_recv()
        gather_hop(half, part, 2).start()
        gather_hop(half, part, 1).wait_recv()
        gather_hop(half, part, 3).start()

    def project(half, part):
        gather_hop(half, part, 2).wait_recv()
        gather_hop(half, part, 3).wait_recv()
        starts = [
            pl.multiple_of(owner * width + part * part_width, part_width)
            for owner in (t, left, right, across)
        ]

        def add(i, value):
            if part > 0:
                value = total[i] + value
            if part < PARTS - 1:
                total[i] = value
            else:
                heads[i] = value.astype(BF16)

        for i, w in enumerate((wq, wk, wv)):
            value = None
            for k in range(4):
                more = product(xin[half, part, k, 0], w[pl.ds(starts[k], part_width), :])
                value = more if value is None else value + more
            add(i, value)
        value = None
        for k in range(4):
            more = product(xin[half, part, k, 1], wo[:, pl.ds(starts[k], part_width)], (1, 1))
            value = more if value is None else value + more
        add(3, value)

    def attend(half):
        scale = HEAD_DIM ** (-0.5)
        usable = count[half, :1, :1] > iota((1, CAP), 1).astype(F32)

        @pl.loop(0, width // HEAD_DIM)
        def _(h):
            at = pl.ds(pl.multiple_of(h * HEAD_DIM, HEAD_DIM), HEAD_DIM)
            query, key_rows, value_rows, grad_rows = (heads[i, :, at] for i in range(4))
            scores = product(query, key_rows, (1, 1)) * scale
            scores = jnp.where(usable, scores, -1e30)
            raised = jnp.exp(scores - jnp.max(scores, axis=1, keepdims=True))
            probs = raised / jnp.sum(raised, axis=1, keepdims=True)
            rounded = probs.astype(BF16)
            grad_probs = product(grad_rows, value_rows, (1, 1))
            inner = jnp.sum(grad_probs * probs, axis=1, keepdims=True)
            grad_scores = (probs * (grad_probs - inner) * scale).astype(BF16)
            heads[4, :, at] = product(rounded, value_rows).astype(BF16)
            heads[5, :, at] = product(grad_scores, key_rows).astype(BF16)
            heads[6, :, at] = product(grad_scores, query, (0, 0)).astype(BF16)
            heads[7, :, at] = product(rounded, grad_rows, (0, 0)).astype(BF16)

    def out_part(target, part):
        start = pl.multiple_of(target * width + part * part_width, part_width)
        return product(heads[4], wo[:, pl.ds(start, part_width)])

    def grad_part(target, part):
        start = pl.multiple_of(target * width + part * part_width, part_width)
        rows = pl.ds(start, part_width)
        return (
            product(heads[5], wq[rows, :], (1, 1))
            + product(heads[6], wk[rows, :], (1, 1))
            + product(heads[7], wv[rows, :], (1, 1))
        )

    def outputs(half, part):
        for i, target, make in (
            (0, across, out_part),
            (1, across, grad_part),
            (4, right, grad_part),
            (5, left, out_part),
        ):
            sums_out[half, part, i] = make(target, part).astype(BF16)
            sum_hop(half, part, i).start()
        own[half, part, 2] = out_part(right, part)
        own[half, part, 3] = grad_part(left, part)
        own[half, part, 0] = out_part(t, part)
        own[half, part, 1] = grad_part(t, part)

    def combine(half, part):
        for i in (2, 3):
            sum_hop(half, part, i - 2).wait_recv()
            more = sums_in[half, part, i - 2].astype(F32)
            sums_out[half, part, i] = (own[half, part, i] + more).astype(BF16)
            sum_hop(half, part, i).start()

    def finish(half, part):
        for i in range(2, 6):
            sum_hop(half, part, i).wait_recv()
        arrived = [sums_in[half, part, i].astype(F32) for i in range(2, 6)]
        out = own[half, part, 0] + arrived[0] + arrived[3]
        grad = own[half, part, 1] + arrived[1] + arrived[2]
        both = jnp.concatenate([out.astype(BF16), grad.astype(BF16)], axis=0)

        @pl.loop(0, slots // tile)
        def _(i):
            rows = product(choose[half, pl.ds(i * tile, tile), :], both).astype(BF16)
            expanded[half, part, pl.ds(i * (tile // PAIR), tile // PAIR)] = rows.reshape(
                tile // PAIR, PAIR, part_width
            )

        send_all(half, part, expanded, back, back_send, back_recv)

    def unpack(half, part):
        wait_all(half, part, back, back_recv)
        rows = back[half, part].reshape(slots, part_width)
        at = pl.ds(part * part_width, part_width)
        out = product(take[half, 0], rows)
        grad = product(take[half, 1], rows)
        if half == 0:
            attended[:, at] = out.astype(BF16)
            grad_normed[:, at] = grad
        else:
            attended[:, at] = (attended[:, at].astype(F32) + out).astype(BF16)
            grad_normed[:, at] = grad_normed[:, at] + grad

    everything = [(half, part) for half in range(2) for part in range(PARTS)]
    pack(0)
    pl.semaphore_wait(barrier, peers - 1 + ring - 1)
    for part in range(PARTS):
        send_all(0, part, packed, recv, go_send, go_recv)
    pack(1)
    for part in range(PARTS):
        send_all(1, part, packed, recv, go_send, go_recv)

    @pl.loop(0, slots // tile)
    def _(i):
        row, other_row = iota((tile, slots), 0) + i * tile, iota((tile, slots), 1)
        number = (row >> 4) * MOST + (row & (MOST - 1))
        other = (other_row >> 4) * MOST + (other_row & (MOST - 1))
        before[pl.ds(i * tile, tile), :] = (other < number).astype(BF16)

    place_column = column(place_row)
    for half in range(2):
        lane = iota((tokens, slots), 1) + half * slots
        take[half, 0] = (lane == place_column).astype(BF16)
        take[half, 1] = (lane == place_column + MOST).astype(BF16)

    for copy in weights:
        copy.wait()

    compact(0, 0)
    relay(0, 0)
    compact(0, 1)
    project(0, 0)
    relay(0, 1)
    compact(1, 0)
    project(0, 1)
    relay(1, 0)
    attend(0)
    outputs(0, 0)
    compact(1, 1)
    combine(0, 0)
    outputs(0, 1)
    relay(1, 1)
    finish(0, 0)
    combine(0, 1)
    project(1, 0)
    finish(0, 1)
    project(1, 1)
    attend(1)
    outputs(1, 0)
    outputs(1, 1)
    combine(1, 0)
    combine(1, 1)
    finish(1, 0)
    finish(1, 1)
    for half, part in everything:
        unpack(half, part)

    for half, part in everything:
        wait_sent(half, part, packed, go_send)
        wait_sent(half, part, expanded, back_send)
        for i in range(4):
            gather_hop(half, part, i).wait_send()
        for i in range(6):
            sum_hop(half, part, i).wait_send()


def body(normed, cluster, w_query, w_key, w_value, w_out, grad_out):
    peers, ring = lax.axis_size("seq"), lax.axis_size("tp")
    tokens, width = normed.shape
    slots = peers * PAIR
    part_width = width // PARTS
    vmem = pl.BlockSpec(memory_space=pltpu.VMEM)
    anywhere = pl.BlockSpec(memory_space=pl.ANY)
    dma = pltpu.SemaphoreType.DMA
    return pl.pallas_call(
        functools.partial(kernel, peers, ring),
        out_shape=(
            jax.ShapeDtypeStruct((tokens, width), BF16),
            jax.ShapeDtypeStruct((tokens, width), F32),
        ),
        in_specs=[vmem] * 3 + [anywhere] * 4,
        out_specs=(vmem, vmem),
        scratch_shapes=[
            pltpu.VMEM(w_query.shape, BF16),
            pltpu.VMEM(w_key.shape, BF16),
            pltpu.VMEM(w_value.shape, BF16),
            pltpu.VMEM(w_out.shape, BF16),
            pltpu.VMEM((2, PARTS, peers, PAIR, part_width), BF16),
            pltpu.VMEM((2, PARTS, peers, PAIR, part_width), BF16),
            pltpu.VMEM((2, PARTS, peers, PAIR, part_width), BF16),
            pltpu.VMEM((2, PARTS, peers, PAIR, part_width), BF16),
            pltpu.VMEM((2, PARTS, ring, 2, CAP, part_width), BF16),
            pltpu.VMEM((2, PARTS, 6, CAP, part_width), BF16),
            pltpu.VMEM((2, PARTS, 6, CAP, part_width), BF16),
            pltpu.VMEM((slots, slots), BF16),
            pltpu.VMEM((2, slots, 2 * CAP), BF16),
            pltpu.VMEM((2, 2 * CAP, slots), BF16),
            pltpu.VMEM((2, 2, tokens, slots), BF16),
            pltpu.VMEM((2, 8, 128), F32),
            pltpu.VMEM((8, CAP, width), BF16),
            pltpu.VMEM((4, CAP, width), F32),
            pltpu.VMEM((2, PARTS, 4, CAP, part_width), F32),
            dma((4,)),
            dma((2, PARTS)),
            dma((2, PARTS)),
            dma((2, PARTS)),
            dma((2, PARTS)),
            dma((2, PARTS, 4)),
            dma((2, PARTS, 4)),
            dma((2, PARTS, 6)),
            dma((2, PARTS, 6)),
        ],
        compiler_params=pltpu.CompilerParams(
            collective_id=0, has_side_effects=True, vmem_limit_bytes=60 * 2**20
        ),
        name="routed",
    )(cluster.reshape(1, tokens), normed, grad_out, w_query, w_key, w_value, w_out)


def solution(mesh):
    in_specs = (
        P("seq", "tp"),
        P("seq", None),
        P(None, "tp"),
        P(None, "tp"),
        P(None, "tp"),
        P("tp", None),
        P("seq", "tp"),
    )
    out_specs = (P("seq", "tp"), P("seq", "tp"))
    return jax.shard_map(body, mesh=mesh, in_specs=in_specs, out_specs=out_specs, check_vma=False)
```

time: 169 us -> 151 us (0.89)
  Pallas kernels: 162 us -> 146 us
    pallas_call x1, Pallas kernels: 162 us -> 146 us  [body(): pl.pallas_call(functools.partial(kernel, peers, ring), out_shape=(jax.Sha...]
    unnamed x3 -> x2, local copies, waits for them, and re-layouts: 5.67 us -> 4.13 us
where the time goes in v3:
time: 151 us
  Pallas kernels  146 us (97%)
  local copies, waits for them, and re-layouts  4.13 us (3%)
    pallas_call x1, Pallas kernels, body(): pl.pallas_call(functools.partial(kernel, peers, ring), out_shape=(jax.Sha...  146 us
    unnamed x2, local copies, waits for them, and re-layouts  4.13 us

profile of v3, /device:TPU:1, one launch (start us, length us, event | category | flops | bytes accessed | tf_op | source)
XLA Modules:
  0.0 151.1 jit_solution(10205858845091322347)
XLA Ops:
  0.6 146.3 %routed.1 = (bf16[512,512]{1,0:T(8,128)(2,1)}, f32[512,512]{1,0:T(8,128)}) custom-call(s32[1,512]{1,0:T(1,128)} %bitcast.1, bf16[512,512]{1,0:T(8,128)(2,1)} %normed.1, bf16[512,512]{1,0:T(8,128)(2,1)} %grad_out.1, bf16[2048,512]{1,0:T(8,128)(2,1)} %wq_hbm.1, bf16[2048,512]{1,0:T(8,128)(2,1)} %wk_hbm.1, bf16[2048,512]{1,0:T(8,128)(2,1)} %wv_hbm.1, ...), custom_call_target="tpu_custom_call" | custom-call | tf_op jit(solution)/shard_map/routed/pallas_call | solution.py:404
  146.9 1.9 %copy.11 = bf16[512,512]{1,0:T(8,128)(2,1)} copy(bf16[512,512]{1,0:T(8,128)(2,1)} %get-tuple-element.4) | data formatting | bytes 1048576
  148.8 2.3 %copy.12 = f32[512,512]{1,0:T(8,128)} copy(f32[512,512]{1,0:T(8,128)} %get-tuple-element.5) | data formatting | bytes 2097152

commit v4 on v3

--- a/solution.py
+++ b/solution.py
@@ -39,8 +39,7 @@
     wk_hbm,
     wv_hbm,
     wo_hbm,
-    attended,
-    grad_normed,
+    result,
     wq,
     wk,
     wv,
@@ -175,12 +174,13 @@
         return hop(src, dst, x_send.at[half, part, i], x_recv.at[half, part, i], target)
 
     def sum_hop(half, part, i):
+        target = (right, left)[i % 2]
         return hop(
             sums_out.at[half, part, i],
             sums_in.at[half, part, i],
             r_send.at[half, part, i],
             r_recv.at[half, part, i],
-            (right, left)[i % 2],
+            target,
         )
 
     def rank_slots(half):
@@ -208,14 +208,13 @@
         rows = recv[half, part].reshape(slots, part_width)
         both = product(gather_rows[half], rows).astype(BF16)
         xin[half, part, 0] = both.reshape(2, CAP, part_width)
-        gather_hop(half, part, 0).start()
-        gather_hop(half, part, 1).start()
+        for i in range(2):
+            gather_hop(half, part, i).start()
 
     def relay(half, part):
-        gather_hop(half, part, 0).wait_recv()
-        gather_hop(half, part, 2).start()
-        gather_hop(half, part, 1).wait_recv()
-        gather_hop(half, part, 3).start()
+        for i in range(2):
+            gather_hop(half, part, i).wait_recv()
+            gather_hop(half, part, 2 + i).start()
 
     def project(half, part):
         gather_hop(half, part, 2).wait_recv()
@@ -249,7 +248,7 @@
         scale = HEAD_DIM ** (-0.5)
         usable = count[half, :1, :1] > iota((1, CAP), 1).astype(F32)
 
-        @pl.loop(0, width // HEAD_DIM)
+        @pl.loop(0, width // HEAD_DIM, unroll=4)
         def _(h):
             at = pl.ds(pl.multiple_of(h * HEAD_DIM, HEAD_DIM), HEAD_DIM)
             query, key_rows, value_rows, grad_rows = (heads[i, :, at] for i in range(4))
@@ -288,8 +287,8 @@
         ):
             sums_out[half, part, i] = make(target, part).astype(BF16)
             sum_hop(half, part, i).start()
-        own[half, part, 2] = out_part(right, part)
-        own[half, part, 3] = grad_part(left, part)
+        for i, target, make in ((2, right, out_part), (3, left, grad_part)):
+            own[half, part, i] = make(target, part)
         own[half, part, 0] = out_part(t, part)
         own[half, part, 1] = grad_part(t, part)
 
@@ -303,9 +302,13 @@
     def finish(half, part):
         for i in range(2, 6):
             sum_hop(half, part, i).wait_recv()
-        arrived = [sums_in[half, part, i].astype(F32) for i in range(2, 6)]
-        out = own[half, part, 0] + arrived[0] + arrived[3]
-        grad = own[half, part, 1] + arrived[1] + arrived[2]
+        out, grad = own[half, part, 0], own[half, part, 1]
+        for i in range(2, 6):
+            more = sums_in[half, part, i].astype(F32)
+            if i in (2, 5):
+                out = out + more
+            else:
+                grad = grad + more
         both = jnp.concatenate([out.astype(BF16), grad.astype(BF16)], axis=0)
 
         @pl.loop(0, slots // tile)
@@ -323,12 +326,10 @@
         at = pl.ds(part * part_width, part_width)
         out = product(take[half, 0], rows)
         grad = product(take[half, 1], rows)
-        if half == 0:
-            attended[:, at] = out.astype(BF16)
-            grad_normed[:, at] = grad
-        else:
-            attended[:, at] = (attended[:, at].astype(F32) + out).astype(BF16)
-            grad_normed[:, at] = grad_normed[:, at] + grad
+        for i, value in enumerate((out, grad)):
+            if half == 1:
+                value = result[i, :, at].astype(F32) + value
+            result[i, :, at] = value.astype(BF16)
 
     everything = [(half, part) for half in range(2) for part in range(PARTS)]
     pack(0)
@@ -356,33 +357,35 @@
         copy.wait()
 
     compact(0, 0)
+    compact(0, 1)
     relay(0, 0)
-    compact(0, 1)
-    project(0, 0)
     relay(0, 1)
     compact(1, 0)
+    project(0, 0)
     project(0, 1)
-    relay(1, 0)
     attend(0)
     outputs(0, 0)
+    outputs(0, 1)
+    combine(0, 0)
     compact(1, 1)
-    combine(0, 0)
-    outputs(0, 1)
-    relay(1, 1)
     finish(0, 0)
     combine(0, 1)
+    relay(1, 0)
+    relay(1, 1)
+    finish(0, 1)
     project(1, 0)
-    finish(0, 1)
     project(1, 1)
     attend(1)
     outputs(1, 0)
+    combine(1, 0)
     outputs(1, 1)
-    combine(1, 0)
+    finish(1, 0)
+    unpack(0, 0)
+    unpack(0, 1)
     combine(1, 1)
-    finish(1, 0)
     finish(1, 1)
-    for half, part in everything:
-        unpack(half, part)
+    unpack(1, 0)
+    unpack(1, 1)
 
     for half, part in everything:
         wait_sent(half, part, packed, go_send)
@@ -401,14 +404,11 @@
     vmem = pl.BlockSpec(memory_space=pltpu.VMEM)
     anywhere = pl.BlockSpec(memory_space=pl.ANY)
     dma = pltpu.SemaphoreType.DMA
-    return pl.pallas_call(
+    result = pl.pallas_call(
         functools.partial(kernel, peers, ring),
-        out_shape=(
-            jax.ShapeDtypeStruct((tokens, width), BF16),
-            jax.ShapeDtypeStruct((tokens, width), F32),
-        ),
+        out_shape=jax.ShapeDtypeStruct((2, tokens, width), BF16),
         in_specs=[vmem] * 3 + [anywhere] * 4,
-        out_specs=(vmem, vmem),
+        out_specs=vmem,
         scratch_shapes=[
             pltpu.VMEM(w_query.shape, BF16),
             pltpu.VMEM(w_key.shape, BF16),
@@ -444,6 +444,7 @@
         ),
         name="routed",
     )(cluster.reshape(1, tokens), normed, grad_out, w_query, w_key, w_value, w_out)
+    return (result[0], result[1].astype(F32))
 
 
 def solution(mesh):

time: 151 us -> 138 us (0.914)
  Pallas kernels: 146 us -> 134 us
  local copies, waits for them, and re-layouts: 4.13 us -> 0 us
  other arithmetic: 0 us -> 2.51 us
    pallas_call x1, Pallas kernels: 146 us -> 134 us  [body(): pl.pallas_call(functools.partial(kernel, peers, ring), out_shape=jax.Shap...]
    unnamed x2 -> x0, local copies, waits for them, and re-layouts: 4.13 us -> none
    convert_element_type x0 -> x1, other arithmetic: none -> 2.51 us  [body(): return (result[0], result[1].astype(F32))]
where the time goes in v4:
time: 138 us; the launch traced here: 137 us
  Pallas kernels  134 us (97%)
  other arithmetic  2.51 us (2%)
    pallas_call x1, Pallas kernels, body(): pl.pallas_call(functools.partial(kernel, peers, ring), out_shape=jax.Shap...  134 us

profile of v4, /device:TPU:1, one launch (start us, length us, event | category | flops | bytes accessed | tf_op | source)
XLA Modules:
  0.0 137.4 jit_solution(13547205965223080651)
XLA Ops:
  0.6 134.3 %routed.1 = bf16[2,512,512]{2,1,0:T(8,128)(2,1)} custom-call(s32[1,512]{1,0:T(1,128)} %bitcast.6, bf16[512,512]{1,0:T(8,128)(2,1)} %normed.1, bf16[512,512]{1,0:T(8,128)(2,1)} %grad_out.1, bf16[2048,512]{1,0:T(8,128)(2,1)} %wq_hbm.1, bf16[2048,512]{1,0:T(8,128)(2,1)} %wk_hbm.1, bf16[2048,512]{1,0:T(8,128)(2,1)} %wv_hbm.1, bf16[512,2048]{1,0:T(8,128)(2,1)} %wo_hbm.1), custom_call_target="tpu_custom_call" | custom-call | tf_op jit(solution)/shard_map/routed/pallas_call | solution.py:407
  134.9 2.5 %bitcast_convert_fusion = (f32[512,512]{1,0:T(8,128)}, bf16[512,512]{1,0:T(8,128)(2,1)}) fusion(bf16[2,512,512]{2,1,0:T(8,128)(2,1)} %routed.1), kind=kLoop, calls=%fused_computation | loop fusion | flops 262144 | bytes 2621440 | tf_op jit(solution)/shard_map/convert_element_type | solution.py:447

commit v5 on v4

--- a/solution.py
+++ b/solution.py
@@ -15,7 +15,7 @@
 EMPTY = 128.0
 PAIR = 2 * MOST
 STRIDE = 27
-PARTS = 2
+PARTS = 4
 F32 = jnp.float32
 BF16 = jnp.bfloat16
 
@@ -166,8 +166,10 @@
     def gather_hop(half, part, i):
         block = xin.at[half, part]
         src, dst, target = (
-            (block.at[0], block.at[1], right),
-            (block.at[0], block.at[2], left),
+            (block.at[0, 0], block.at[1, 0], right),
+            (block.at[0, 1], block.at[2, 1], left),
+            (block.at[0, 1], block.at[1, 1], right),
+            (block.at[0, 0], block.at[2, 0], left),
             (block.at[1, 0], block.at[3, 0], right),
             (block.at[2, 1], block.at[3, 1], left),
         )[i]
@@ -208,17 +210,17 @@
         rows = recv[half, part].reshape(slots, part_width)
         both = product(gather_rows[half], rows).astype(BF16)
         xin[half, part, 0] = both.reshape(2, CAP, part_width)
-        for i in range(2):
+        for i in range(4):
             gather_hop(half, part, i).start()
 
     def relay(half, part):
         for i in range(2):
             gather_hop(half, part, i).wait_recv()
-            gather_hop(half, part, 2 + i).start()
+            gather_hop(half, part, 4 + i).start()
 
     def project(half, part):
-        gather_hop(half, part, 2).wait_recv()
-        gather_hop(half, part, 3).wait_recv()
+        for i in range(2, 6):
+            gather_hop(half, part, i).wait_recv()
         starts = [
             pl.multiple_of(owner * width + part * part_width, part_width)
             for owner in (t, left, right, across)
@@ -357,42 +359,69 @@
         copy.wait()
 
     compact(0, 0)
+    relay(0, 0)
     compact(0, 1)
-    relay(0, 0)
     relay(0, 1)
+    compact(0, 2)
+    compact(0, 3)
+    relay(0, 2)
+    relay(0, 3)
     compact(1, 0)
     project(0, 0)
     project(0, 1)
+    project(0, 2)
+    relay(1, 0)
+    project(0, 3)
+    compact(1, 1)
     attend(0)
     outputs(0, 0)
     outputs(0, 1)
+    outputs(0, 2)
+    outputs(0, 3)
     combine(0, 0)
-    compact(1, 1)
+    compact(1, 2)
+    combine(0, 1)
+    combine(0, 2)
+    combine(0, 3)
+    compact(1, 3)
+    relay(1, 1)
+    relay(1, 2)
     finish(0, 0)
-    combine(0, 1)
-    relay(1, 0)
-    relay(1, 1)
     finish(0, 1)
+    finish(0, 2)
+    relay(1, 3)
+    finish(0, 3)
     project(1, 0)
     project(1, 1)
+    project(1, 2)
+    project(1, 3)
     attend(1)
     outputs(1, 0)
     combine(1, 0)
     outputs(1, 1)
+    outputs(1, 2)
     finish(1, 0)
+    combine(1, 1)
+    combine(1, 2)
+    outputs(1, 3)
+    finish(1, 1)
+    finish(1, 2)
     unpack(0, 0)
     unpack(0, 1)
-    combine(1, 1)
-    finish(1, 1)
+    unpack(0, 2)
+    unpack(0, 3)
+    combine(1, 3)
+    finish(1, 3)
     unpack(1, 0)
     unpack(1, 1)
+    unpack(1, 2)
+    unpack(1, 3)
 
     for half, part in everything:
         wait_sent(half, part, packed, go_send)
         wait_sent(half, part, expanded, back_send)
-        for i in range(4):
+        for i in range(6):
             gather_hop(half, part, i).wait_send()
-        for i in range(6):
             sum_hop(half, part, i).wait_send()
 
 
@@ -434,8 +463,8 @@
             dma((2, PARTS)),
             dma((2, PARTS)),
             dma((2, PARTS)),
-            dma((2, PARTS, 4)),
-            dma((2, PARTS, 4)),
+            dma((2, PARTS, 6)),
+            dma((2, PARTS, 6)),
             dma((2, PARTS, 6)),
             dma((2, PARTS, 6)),
         ],

time: 138 us -> 134 us (0.971)
  Pallas kernels: 134 us -> 131 us
    pallas_call x1, Pallas kernels: 134 us -> 131 us  [body(): pl.pallas_call(functools.partial(kernel, peers, ring), out_shape=jax.Shap...]
where the time goes in v5:
time: 134 us
  Pallas kernels  131 us (98%)
  other arithmetic  2.51 us (2%)
    pallas_call x1, Pallas kernels, body(): pl.pallas_call(functools.partial(kernel, peers, ring), out_shape=jax.Shap...  131 us

profile of v5, /device:TPU:1, one launch (start us, length us, event | category | flops | bytes accessed | tf_op | source)
XLA Modules:
  0.0 133.7 jit_solution(4857341583700920553)
XLA Ops:
  0.6 130.6 %routed.1 = bf16[2,512,512]{2,1,0:T(8,128)(2,1)} custom-call(s32[1,512]{1,0:T(1,128)} %bitcast.6, bf16[512,512]{1,0:T(8,128)(2,1)} %normed.1, bf16[512,512]{1,0:T(8,128)(2,1)} %grad_out.1, bf16[2048,512]{1,0:T(8,128)(2,1)} %wq_hbm.1, bf16[2048,512]{1,0:T(8,128)(2,1)} %wk_hbm.1, bf16[2048,512]{1,0:T(8,128)(2,1)} %wv_hbm.1, bf16[512,2048]{1,0:T(8,128)(2,1)} %wo_hbm.1), custom_call_target="tpu_custom_call" | custom-call | tf_op jit(solution)/shard_map/routed/pallas_call | solution.py:436
  131.2 2.5 %bitcast_convert_fusion = (f32[512,512]{1,0:T(8,128)}, bf16[512,512]{1,0:T(8,128)(2,1)}) fusion(bf16[2,512,512]{2,1,0:T(8,128)(2,1)} %routed.1), kind=kLoop, calls=%fused_computation | loop fusion | flops 262144 | bytes 2621440 | tf_op jit(solution)/shard_map/convert_element_type | solution.py:476

commit v6 on v5

--- a/solution.py
+++ b/solution.py
@@ -133,7 +133,7 @@
             src.at[half, part, s], dst.at[half, part, s], recv_sem.at[half, part]
         ).start()
 
-        @pl.loop(1, peers)
+        @pl.loop(1, peers, unroll=7)
         def _(r):
             peer = lax.rem(s + r * STRIDE, peers)
             pltpu.make_async_remote_copy(

time: 134 us -> 134 us (level)
  no operation moved by 1% of the time
where the time goes in v6:
time: 134 us
  Pallas kernels  130 us (97%)
  other arithmetic  2.51 us (2%)
    pallas_call x1, Pallas kernels, body(): pl.pallas_call(functools.partial(kernel, peers, ring), out_shape=jax.Shap...  130 us

profile of v6, /device:TPU:1, one launch (start us, length us, event | category | flops | bytes accessed | tf_op | source)
XLA Modules:
  0.0 133.6 jit_solution(17831802635084395782)
XLA Ops:
  0.6 130.5 %routed.1 = bf16[2,512,512]{2,1,0:T(8,128)(2,1)} custom-call(s32[1,512]{1,0:T(1,128)} %bitcast.6, bf16[512,512]{1,0:T(8,128)(2,1)} %normed.1, bf16[512,512]{1,0:T(8,128)(2,1)} %grad_out.1, bf16[2048,512]{1,0:T(8,128)(2,1)} %wq_hbm.1, bf16[2048,512]{1,0:T(8,128)(2,1)} %wk_hbm.1, bf16[2048,512]{1,0:T(8,128)(2,1)} %wv_hbm.1, bf16[512,2048]{1,0:T(8,128)(2,1)} %wo_hbm.1), custom_call_target="tpu_custom_call" | custom-call | tf_op jit(solution)/shard_map/routed/pallas_call | solution.py:436
  131.1 2.5 %bitcast_convert_fusion = (f32[512,512]{1,0:T(8,128)}, bf16[512,512]{1,0:T(8,128)(2,1)}) fusion(bf16[2,512,512]{2,1,0:T(8,128)(2,1)} %routed.1), kind=kLoop, calls=%fused_computation | loop fusion | flops 262144 | bytes 2621440 | tf_op jit(solution)/shard_map/convert_element_type | solution.py:476
